TPU v7x, 128 devices: a whole 4x4x4 slice. The times are simulated.
128 devices in a mesh: space: 8 (over x_hi, z), rep: 16 (over y, x_lo, core).
Axes of the slice: x: 4 (x_hi: 2, x_lo: 2; x = x_hi * 2 + x_lo), y: 4, z: 4, core: 2. Of those that a mesh axis runs over, the one named last changes fastest.
Arguments:
- features: bfloat16 [16, 40, 96, 1024], P('rep', 'space'), may hold values from -4 to 4.5
- labels: int32 [16, 40, 96], P('rep', 'space'), may hold values from 0 to 2
- w_in: bfloat16 [29, 1024, 256], replicated, may hold values from -0.0625 to 0.0625
- w_proj: bfloat16 [1280, 256], replicated, may hold values from -0.15625 to 0.15625
- w_cls: bfloat16 [256, 3], replicated, may hold values from -0.375 to 0.375
- class_weight: float32 [3], replicated, may hold values from 0.5 to 4
- matching: int32 [16], replicated, may hold values from 0 to 15, as said below
Outputs:
- avg_in: float32 [16, 29696, 256], P('rep', 'space')
- avg_proj: float32 [16, 1280, 256], P('rep', 'space')
- avg_cls: float32 [16, 256, 3], P('rep', 'space')
Inputs may be any that keep to these rules, and one draw needn't show every extreme that they name: matching[i] = i XOR matching[0] with matching[0] nonzero, so replicas are matched in pairs.
All inputs are finite; a program needn't handle non-finite values.
Results may differ from a plain program's by a relative error of at most 0.025.
The roundings to bfloat16 on the way count: a program that leaves them out, or rounds other values in their place, can miss the bound.
Values may be sent and summed in bfloat16 or wider, within the bound.
A program may use at most 256 MiB of HBM per device.

v0:
```python
import jax
import jax.numpy as jnp
from jax import lax
from jax.sharding import PartitionSpec as P

loss_scale = 1024.0


def from_partner(value, axis, apart):
    mask = 2**apart
    pairs = [(source, source ^ mask) for source in range(lax.axis_size(axis))]
    return lax.ppermute(value, axis, pairs)


def shifted(values, offset, along):
    length = values.shape[along]
    extent = abs(offset)
    padding = [(0, 0)] * values.ndim
    padding[along] = (extent, extent)
    return lax.slice_in_dim(
        jnp.pad(values, padding), extent + offset, extent + offset + length, axis=along
    )


def contract(left, right):
    return lax.dot_general(
        left, right, (((0,), (0,)), ((), ())), preferred_element_type=jnp.float32
    )


def per_device(features, labels, w_in, w_proj, w_cls, class_weight, matching):
    field_map = features[0]
    label_map = labels[0]
    rows_dev, col_count, in_width = field_map.shape
    out_width = w_proj.shape[1]
    space_size = lax.axis_size("space")
    space_index = lax.axis_index("space")
    pixels = rows_dev * col_count
    total_pix = pixels * space_size
    flat_rows = field_map.reshape(pixels, in_width)
    column_sum = jnp.sum(field_map, axis=(0, 1), dtype=jnp.float32)
    mean_in = (lax.psum(column_sum, "space") / total_pix).astype(jnp.bfloat16)
    offsets = [-36, -24, -12, 12, 24, 36]
    whole_map = None
    whole_map = lax.all_gather(field_map, "space", axis=0, tiled=True)
    padded = jnp.pad(whole_map, ((36, 36), (0, 0), (0, 0)))
    row_views = {
        offset: lax.dynamic_slice_in_dim(padded, space_index * rows_dev + 36 + offset, rows_dev, 0)
        for offset in offsets
    }
    row_views[0] = field_map
    pre_list = [jnp.dot(flat_rows, w_in[0], preferred_element_type=jnp.float32)]
    for k in range(1, 4):
        dilation = 12 * k
        pre_act = jnp.zeros((rows_dev, col_count, out_width), jnp.float32)
        for i in range(3):
            row_block = row_views[(i - 1) * dilation].reshape(pixels, in_width)
            for j in range(3):
                product = jnp.dot(
                    row_block, w_in[1 + 9 * (k - 1) + 3 * i + j], preferred_element_type=jnp.float32
                )
                pre_act = pre_act + shifted(
                    product.reshape(rows_dev, col_count, out_width), (j - 1) * dilation, 1
                )
        pre_list.append(pre_act.reshape(pixels, out_width))
    pool_pre = jnp.dot(mean_in[None, :], w_in[28], preferred_element_type=jnp.float32)
    act_list = [jax.nn.relu(p).astype(jnp.bfloat16) for p in pre_list]
    pool_act = jnp.broadcast_to(jax.nn.relu(pool_pre).astype(jnp.bfloat16), (pixels, out_width))
    concat = jnp.concatenate(act_list + [pool_act], axis=1)
    y_pre = jnp.dot(concat, w_proj, preferred_element_type=jnp.float32)
    y_act = jax.nn.relu(y_pre).astype(jnp.bfloat16)
    logits = jnp.dot(y_act, w_cls, preferred_element_type=jnp.float32)
    exp_logits = jnp.exp(logits)
    softmax_out = exp_logits / jnp.sum(exp_logits, axis=1, keepdims=True)
    onehot = (
        label_map.reshape(pixels)[:, None] == jnp.arange(logits.shape[1], dtype=jnp.int32)[None, :]
    ).astype(jnp.float32)
    weight = jnp.sum(onehot * class_weight[None, :], axis=1)
    d_logits = ((softmax_out - onehot) * weight[:, None] * (loss_scale / total_pix)).astype(
        jnp.bfloat16
    )
    g_cls = contract(y_act, d_logits)
    d_y = (jnp.dot(d_logits, w_cls.T, preferred_element_type=jnp.float32) * (y_pre > 0)).astype(
        jnp.bfloat16
    )
    g_proj = contract(concat, d_y)
    d_cat = jnp.dot(d_y, w_proj.T, preferred_element_type=jnp.float32)
    d_list = []
    for k in range(4):
        d_branch = (d_cat[:, k * out_width : (k + 1) * out_width] * (pre_list[k] > 0)).astype(
            jnp.bfloat16
        )
        d_list.append(d_branch.reshape(rows_dev, col_count, out_width))
    s_pool = jnp.sum(d_cat[:, 4 * out_width :] * (pool_pre > 0), axis=0)
    grad_list = [contract(flat_rows, d_list[0].reshape(pixels, out_width))]
    for k in range(1, 4):
        dilation = 12 * k
        for i in range(3):
            row_block = row_views[(i - 1) * dilation].reshape(pixels, in_width)
            for j in range(3):
                moved_grad = shifted(d_list[k], -(j - 1) * dilation, 1).reshape(pixels, out_width)
                grad_list.append(contract(row_block, moved_grad))
    grad_list.append(mean_in.astype(jnp.float32)[:, None] * s_pool[None, :])
    g_in = jnp.stack(grad_list).reshape(-1, out_width)
    sum_in, sum_proj, sum_cls = (
        lax.psum_scatter(
            g_in.astype(jnp.bfloat16), "space", scatter_dimension=0, tiled=True
        ).astype(jnp.float32),
        lax.psum_scatter(
            g_proj.astype(jnp.bfloat16), "space", scatter_dimension=0, tiled=True
        ).astype(jnp.float32),
        lax.psum_scatter(
            g_cls.astype(jnp.bfloat16), "space", scatter_dimension=0, tiled=True
        ).astype(jnp.float32),
    )
    share_in = sum_in.astype(jnp.bfloat16)
    share_proj = sum_proj.astype(jnp.bfloat16)
    share_cls = sum_cls.astype(jnp.bfloat16)
    own_grad = jnp.concatenate(
        [share_in.reshape(-1), share_proj.reshape(-1), share_cls.reshape(-1)]
    )
    pair_bits = matching[0]
    partner_grad = own_grad
    for b in range(lax.axis_size("rep").bit_length() - 1):
        swapped = from_partner(partner_grad, "rep", b)
        bit_on = jnp.bitwise_and(jnp.right_shift(pair_bits, b), 1) == 1
        partner_grad = jnp.where(bit_on, swapped, partner_grad)
    partner_full = partner_grad.astype(jnp.float32)
    averaged = (own_grad.astype(jnp.float32) + partner_full) * 0.5
    size_in = share_in.size
    size_proj = share_proj.size
    avg_in = averaged[:size_in].reshape(share_in.shape)
    avg_proj = averaged[size_in : size_in + size_proj].reshape(share_proj.shape)
    avg_cls = averaged[size_in + size_proj :].reshape(share_cls.shape)
    return (avg_in[None], avg_proj[None], avg_cls[None])


def solution(mesh):
    return jax.shard_map(
        per_device,
        mesh=mesh,
        in_specs=(P("rep", "space", None, None), P("rep", "space", None), P(), P(), P(), P(), P()),
        out_specs=(P("rep", "space", None), P("rep", "space", None), P("rep", "space", None)),
        check_vma=False,
    )
```

profile of v0, /device:TPU:1, one launch (start us, length us, event | category | flops | bytes accessed | tf_op | source)
XLA Modules:
  0.0 636.6 jit_solution(8254590426877515783)
XLA Ops:
  10.1 22.7 %psum.7 = f32[1024]{0:T(1024)S(1)} all-reduce(f32[1024]{0:T(1024)S(1)} %convert_reduce_fusion), channel_id=1, replica_groups=mesh['space'=8,'rep'=16] {'space'}, use_global_device_ids=true, to_apply=%region_1.0 | all-reduce | flops 1024 | bytes 8192 | tf_op jit(solution)/shard_map/psum | solution.py:42
  34.8 2.5 fusion.97
  37.4 2.6 fusion.94
  40.0 2.6 fusion.92
  42.6 1.8 fusion.89
  44.3 2.6 fusion.87
  46.9 2.6 fusion.84
  49.4 2.6 fusion.177
  52.1 63.7 %all-gather.3.cloned.1.call-done = bf16[1,40,96,1024]{3,2,0,1:T(8,128)(2,1)} async-done(((bf16[1,5,96,1024]{3,2,0,1:T(8,128)(2,1)}), bf16[1,40,96,1024]{3,2,0,1:T(8,128)(2,1)}) %all-gather.3.cloned.1.call-update) | async-done | bytes 7864336 | tf_op jit(solution)/shard_map/all_gather | solution.py:45
  115.8 3.5 pad_dynamic-slice_fusion
  119.4 2.0 fusion.102
  121.4 1.9 fusion.105
  123.3 1.5 fusion.128
  124.8 1.5 fusion.131
  126.3 1.5 fusion.123
  127.8 1.5 fusion.126
  129.2 1.5 fusion.115
  130.7 1.5 fusion.118
  132.3 1.5 fusion.110
  133.7 1.5 fusion.113
  135.3 1.5 fusion.136
  136.7 1.5 fusion.139
  138.2 1.6 fusion.82
  139.9 1.5 fusion.81
  141.3 2.3 maximum_convert_fusion.3
  145.1 1.5 fusion.79
  146.6 1.5 maximum_convert_fusion.2
  148.1 1.5 fusion.78
  149.6 1.5 fusion.77
  151.0 2.3 maximum_convert_fusion.1
  154.6 1.6 convolution_convert_fusion
  156.2 2.0 fusion.186
  161.4 1.6 fusion.173
  163.2 2.5 fusion.13
  165.6 2.6 fusion.67
  168.2 2.5 fusion.15
  170.7 2.5 fusion.65
  206.3 20.5 %copy.70 = bf16[29,1024,256]{2,1,0:T(8,128)(2,1)} copy(bf16[29,1024,256]{1,2,0:T(8,128)(2,1)} %fusion.99) | data formatting | bytes 30408704 | tf_op jit(solution)/shard_map/stack | solution.py:104
  227.6 72.2 %reduce-scatter.8.cloned.1.call-done = bf16[160,256]{1,0:T(8,128)(2,1)} async-done(((bf16[1280,256]{1,0:T(8,128)(2,1)}), bf16[160,256]{1,0:T(8,128)(2,1)}) %reduce-scatter.8.cloned.1.call-update) | async-done | bytes 81936 | tf_op jit(solution)/shard_map/reduce_scatter | solution.py:109
  300.8 178.5 %reduce-scatter.6.cloned.1.call-done = bf16[3712,256]{1,0:T(8,128)(2,1)} async-done(((bf16[29696,256]{1,0:T(8,128)(2,1)}), bf16[3712,256]{1,0:T(8,128)(2,1)}) %reduce-scatter.6.cloned.1.call-update) | async-done | bytes 1900560 | tf_op jit(solution)/shard_map/reduce_scatter | solution.py:106
  479.3 3.5 copy.105
  484.3 3.6 collective-permute-done
  488.5 44.1 %collective-permute-done.1 = bf16[991328]{0:T(1024)(128)(2,1)S(1)} collective-permute-done((bf16[991328]{0:T(1024)(128)(2,1)S(1)}, bf16[991328]{0:T(1024)(128)(2,1)S(1)}, u32[]{:S(2)}, u32[]{:S(2)}) %collective-permute-start.1) | collective-permute-done | bytes 1982688 | tf_op jit(solution)/shard_map/ppermute | solution.py:12
  534.1 42.3 %collective-permute-done.2 = bf16[991328]{0:T(1024)(128)(2,1)S(1)} collective-permute-done((bf16[991328]{0:T(1024)(128)(2,1)S(1)}, bf16[991328]{0:T(1024)(128)(2,1)S(1)}, u32[]{:S(2)}, u32[]{:S(2)}) %collective-permute-start.2) | collective-permute-done | bytes 1982688 | tf_op jit(solution)/shard_map/ppermute | solution.py:12
  576.6 2.8 collective-permute-start.3
  579.5 41.3 %collective-permute-done.3 = bf16[991328]{0:T(1024)(128)(2,1)S(1)} collective-permute-done((bf16[991328]{0:T(1024)(128)(2,1)S(1)}, bf16[991328]{0:T(1024)(128)(2,1)S(1)}, u32[]{:S(2)}, u32[]{:S(2)}) %collective-permute-start.3) | collective-permute-done | bytes 1982688 | tf_op jit(solution)/shard_map/ppermute | solution.py:12
  621.5 2.1 slice.265
  624.3 5.0 broadcast_in_dim_reshape.9
  (116 shorter events, 51.9 us)
Async XLA Ops:
  7.2 146.2 %copy-start = (bf16[1280,256]{1,0:T(8,128)(2,1)S(1)}, bf16[1280,256]{1,0:T(8,128)(2,1)}, u32[]{:S(2)}) copy-start(bf16[1280,256]{1,0:T(8,128)(2,1)} %param.10) | copy-start | bytes 1966084
  7.2 108.6 %all-gather.3.cloned.1.call-start = ((), (), s32[]{:S(2)}) async-start(), calls=%async_computation.5 | async-start | bytes 8847360 | tf_op jit(solution)/shard_map/all_gather | solution.py:45
  7.9 218.9 %reduce-scatter.10.cloned.1.call-start = ((), (), s32[]{:S(2)}) async-start(), calls=%async_computation.6 | async-start | bytes 73728 | tf_op jit(solution)/shard_map/reduce_scatter | solution.py:112
  119.3 22.0 %copy-start.5 = (bf16[5,96,1024]{2,1,0:T(8,128)(2,1)}, bf16[5,96,1024]{2,1,0:T(8,128)(2,1)S(1)}, u32[]{:S(2)}) copy-start(bf16[5,96,1024]{2,1,0:T(8,128)(2,1)S(1)} %get-tuple-element.15) | copy-start | bytes 2949124
  119.3 22.0 %copy-start.11 = (bf16[5,96,1024]{2,1,0:T(8,128)(2,1)}, bf16[5,96,1024]{2,1,0:T(8,128)(2,1)S(1)}, u32[]{:S(2)}) copy-start(bf16[5,96,1024]{2,1,0:T(8,128)(2,1)S(1)} %get-tuple-element.19) | copy-start | bytes 2949124
  119.3 24.3 %copy-start.9 = (bf16[5,96,1024]{2,1,0:T(8,128)(2,1)}, bf16[5,96,1024]{2,1,0:T(8,128)(2,1)S(1)}, u32[]{:S(2)}) copy-start(bf16[5,96,1024]{2,1,0:T(8,128)(2,1)S(1)} %get-tuple-element.16) | copy-start | bytes 2949124
  119.3 27.3 %copy-start.3 = (bf16[5,96,1024]{2,1,0:T(8,128)(2,1)}, bf16[5,96,1024]{2,1,0:T(8,128)(2,1)S(1)}, u32[]{:S(2)}) copy-start(bf16[5,96,1024]{2,1,0:T(8,128)(2,1)S(1)} %get-tuple-element.17) | copy-start | bytes 2949124
  119.3 28.7 %copy-start.7 = (bf16[5,96,1024]{2,1,0:T(8,128)(2,1)}, bf16[5,96,1024]{2,1,0:T(8,128)(2,1)S(1)}, u32[]{:S(2)}) copy-start(bf16[5,96,1024]{2,1,0:T(8,128)(2,1)S(1)} %get-tuple-element.18) | copy-start | bytes 2949124
  119.3 18.9 %copy-start.17 = (f32[5,96,256]{2,1,0:T(8,128)S(1)}, f32[5,96,256]{2,1,0:T(8,128)}, u32[]{:S(2)}) copy-start(f32[5,96,256]{2,1,0:T(8,128)} %fusion.97) | copy-start | bytes 1474564
  119.3 20.5 %copy-start.2 = (bf16[1,5,96,1024]{3,2,1,0:T(8,128)(2,1)S(1)}, bf16[1,5,96,1024]{3,2,1,0:T(8,128)(2,1)}, u32[]{:S(2)}) copy-start(bf16[1,5,96,1024]{3,2,1,0:T(8,128)(2,1)} %param.7) | copy-start | bytes 2949124
  119.4 20.5 %copy-start.16 = (f32[5,96,256]{2,1,0:T(8,128)S(1)}, f32[5,96,256]{2,1,0:T(8,128)}, u32[]{:S(2)}) copy-start(f32[5,96,256]{2,1,0:T(8,128)} %fusion.94) | copy-start | bytes 1474564
  123.3 20.3 %copy-start.15 = (f32[5,96,256]{2,1,0:T(8,128)S(1)}, f32[5,96,256]{2,1,0:T(8,128)}, u32[]{:S(2)}) copy-start(f32[5,96,256]{2,1,0:T(8,128)} %fusion.92) | copy-start | bytes 1474564
  130.7 17.4 %copy-start.14 = (f32[5,96,256]{2,1,0:T(8,128)S(1)}, f32[5,96,256]{2,1,0:T(8,128)}, u32[]{:S(2)}) copy-start(f32[5,96,256]{2,1,0:T(8,128)} %fusion.87) | copy-start | bytes 1474564
  133.7 15.8 %copy-start.13 = (f32[5,96,256]{2,1,0:T(8,128)S(1)}, f32[5,96,256]{2,1,0:T(8,128)}, u32[]{:S(2)}) copy-start(f32[5,96,256]{2,1,0:T(8,128)} %fusion.84) | copy-start | bytes 1474564
  138.2 15.1 %copy-start.12 = (bf16[480,1280]{1,0:T(8,128)(2,1)S(1)}, bf16[480,1280]{1,0:T(8,128)(2,1)}, u32[]{:S(2)}) copy-start(bf16[480,1280]{1,0:T(8,128)(2,1)} %get-tuple-element.29) | copy-start | bytes 3686404
  139.8 14.1 %copy-start.18 = (bf16[256,3]{0,1:T(4,128)(2,1)S(1)}, bf16[256,3]{0,1:T(4,128)(2,1)}, u32[]{:S(2)}) copy-start(bf16[256,3]{0,1:T(4,128)(2,1)} %param.11) | copy-start | bytes 4612
  160.0 139.8 %reduce-scatter.8.cloned.1.call-start = ((), (), s32[]{:S(2)}) async-start(), calls=%async_computation.4 | async-start | bytes 737280 | tf_op jit(solution)/shard_map/reduce_scatter | solution.py:109
  160.1 16.9 %copy-start.6 = (bf16[5,96,1024]{2,1,0:T(8,128)(2,1)S(1)}, bf16[5,96,1024]{2,1,0:T(8,128)(2,1)}, u32[]{:S(2)}) copy-start(bf16[5,96,1024]{2,1,0:T(8,128)(2,1)} %copy-done.5) | copy-start | bytes 2949124
  160.1 20.7 %copy-start.10 = (bf16[5,96,1024]{2,1,0:T(8,128)(2,1)S(1)}, bf16[5,96,1024]{2,1,0:T(8,128)(2,1)}, u32[]{:S(2)}) copy-start(bf16[5,96,1024]{2,1,0:T(8,128)(2,1)} %copy-done.9) | copy-start | bytes 2949124
  165.6 22.8 %copy-start.4 = (bf16[5,96,1024]{2,1,0:T(8,128)(2,1)S(1)}, bf16[5,96,1024]{2,1,0:T(8,128)(2,1)}, u32[]{:S(2)}) copy-start(bf16[5,96,1024]{2,1,0:T(8,128)(2,1)} %copy-done.3) | copy-start | bytes 2949124
  173.2 19.2 %copy-start.8 = (bf16[5,96,1024]{2,1,0:T(8,128)(2,1)S(1)}, bf16[5,96,1024]{2,1,0:T(8,128)(2,1)}, u32[]{:S(2)}) copy-start(bf16[5,96,1024]{2,1,0:T(8,128)(2,1)} %copy-done.7) | copy-start | bytes 2949124
  198.9 280.4 %reduce-scatter.6.cloned.1.call-start = ((), (), s32[]{:S(2)}) async-start(), calls=%async_computation.3 | async-start | bytes 17104896 | tf_op jit(solution)/shard_map/reduce_scatter | solution.py:106
  226.8 257.4 %copy-start.19 = (s32[16]{0:T(128)S(1)}, s32[16]{0:T(128)}, u32[]{:S(2)}) copy-start(s32[16]{0:T(128)} %param.13) | copy-start | bytes 196
  482.9 4.9 collective-permute-start
  488.0 44.5 %collective-permute-start.1 = (bf16[991328]{0:T(1024)(128)(2,1)S(1)}, bf16[991328]{0:T(1024)(128)(2,1)S(1)}, u32[]{:S(2)}, u32[]{:S(2)}) collective-permute-start(bf16[991328]{0:T(1024)(128)(2,1)S(1)} %broadcast_select_fusion), channel_id=1, source_target_pairs={{0,2},{1,3},{2,0},{3,1},{4,6},{5,7},{6,4},{7,5},{8,10},{9,11},{10,... | collective-permute-start | bytes 5947976 | tf_op jit(solution)/shard_map/ppermute | solution.py:12
  532.8 43.6 %collective-permute-start.2 = (bf16[991328]{0:T(1024)(128)(2,1)S(1)}, bf16[991328]{0:T(1024)(128)(2,1)S(1)}, u32[]{:S(2)}, u32[]{:S(2)}) collective-permute-start(bf16[991328]{0:T(1024)(128)(2,1)S(1)} %broadcast_select_fusion.1), channel_id=1, source_target_pairs={{0,4},{1,5},{2,6},{3,7},{4,0},{5,1},{6,2},{7,3},{8,12},{9,13},{10,... | collective-permute-start | bytes 5947976 | tf_op jit(solution)/shard_map/ppermute | solution.py:12
  576.4 53.8 %copy-start.1 = (bf16[1280,256]{1,0:T(8,128)(2,1)S(1)}, bf16[1280,256]{1,0:T(8,128)(2,1)}, u32[]{:S(2)}) copy-start(bf16[1280,256]{1,0:T(8,128)(2,1)} %param.10) | copy-start | bytes 1966084
  576.6 44.2 %collective-permute-start.3 = (bf16[991328]{0:T(1024)(128)(2,1)S(1)}, bf16[991328]{0:T(1024)(128)(2,1)S(1)}, u32[]{:S(2)}, u32[]{:S(2)}) collective-permute-start(bf16[991328]{0:T(1024)(128)(2,1)S(1)} %broadcast_select_fusion.2), channel_id=1, source_target_pairs={{0,8},{1,9},{2,10},{3,11},{4,12},{5,13},{6,14},{7,15},{8,0},{9,1},... | collective-permute-start | bytes 5947976 | tf_op jit(solution)/shard_map/ppermute | solution.py:12
Sparse Core Ops, SparseCore 0:
  10.3 105.4 all-gather.2
  160.1 65.8 reduce-scatter.9
  229.6 70.1 reduce-scatter.7
  304.1 175.1 reduce-scatter.5
where the time goes:
time: 641 us; the launch traced here: 637 us
  waiting for transfers between devices  446 us (70%)
  matrix products  97.5 us (15%)
  local copies, waits for them, and re-layouts  39.1 us (6%)
  blocking collectives  22.7 us (4%)
  between operations  14.5 us (2%)
  other arithmetic  10.2 us (2%)
    reduce_scatter x1, waiting for transfers between devices, per_device(): lax.psum_scatter(g_in.astype(jnp.bfloat16), 'space', scatter_dimension=0,...  179 us
    ppermute x4, waiting for transfers between devices, from_partner(): return lax.ppermute(value, axis, pairs)  131 us
    reduce_scatter x1, waiting for transfers between devices, per_device(): lax.psum_scatter(g_proj.astype(jnp.bfloat16), 'space', scatter_dimension=...  72.2 us
    all_gather x1, waiting for transfers between devices, per_device(): whole_map = lax.all_gather(field_map, 'space', axis=0, tiled=True)  63.7 us
    dot_general x27, matrix products, per_device(): jnp.dot(row_block, w_in[1 + 9 * (k - 1) + 3 * i + j], preferred_element_t...  48.2 us
    dot_general x30, matrix products, contract(): lax.dot_general(left, right, (((0,), (0,)), ((), ())), preferred_element_...  42.5 us
    psum x1, blocking collectives, per_device(): mean_in = (lax.psum(column_sum, 'space') / total_pix).astype(jnp.bfloat16)  22.7 us
    another operation x1, local copies, waits for them, and re-layouts, per_device(): g_in = jnp.stack(grad_list).reshape(-1, out_width)  20.5 us
  transfers between devices with their start and end apart: 8, of which 7 were waited for; matrix products, arithmetic and copies ran while one was open for 14% of the time, Pallas kernels for 0%

commit v1 on v0

v1 whole, which is shorter than its diff:
```python
import functools

import jax
import jax.numpy as jnp
from jax import lax
from jax.experimental import pallas as pl
from jax.experimental.pallas import tpu as pltpu
from jax.sharding import PartitionSpec as P

MESH = pl.DeviceIdType.MESH
F32 = jnp.float32
BF16 = jnp.bfloat16

NS = 8
ROWS_DEV = 5
ROWS = 40
COLS = 96
CIN = 1024
COUT = 256
PIX = ROWS_DEV * COLS
FIELD = ROWS * COLS
TAPS = 28
SHARE = 29 * CIN // NS
PROJ_SHARE = 5 * COUT // NS
CLS_SHARE = COUT // NS
OUT_ROWS = SHARE + PROJ_SHARE + CLS_SHARE
PAD = 36
VMEM_LIMIT = 60 * 2**20
loss_scale = 1024.0


def dot(a, b, dims=((1,), (0,))):
    return lax.dot_general(a, b, (dims, ((), ())), preferred_element_type=F32)


def space_barrier(targets):
    barrier = pltpu.get_barrier_semaphore()
    for t in targets:
        pl.semaphore_signal(barrier, inc=1, device_id={"space": t}, device_id_type=MESH)
    pl.semaphore_wait(barrier, len(targets))


def gather_field(x_ref, xf, ssem, rsem):
    me = lax.axis_index("space")
    core = lax.rem(lax.axis_index("rep"), 2)
    xh, z = me // 4, lax.rem(me, 4)

    def idx(x, zz):
        return x * 4 + lax.rem(zz + 8, 4)

    xo = 1 - xh
    X, ZP, ZM = idx(xo, z), idx(xh, z + 1), idx(xh, z - 1)
    way = 1 - 2 * core

    def part(block, half):
        return pl.ds(block * ROWS_DEV, 3) if half == 0 else pl.ds(block * ROWS_DEV + 3, 2)

    def message(m, block, half, target, own=False):
        rows = part(block, half)
        src = x_ref.at[pl.ds(0, 3) if half == 0 else pl.ds(3, 2)] if own else xf.at[rows]
        return pltpu.make_async_remote_copy(
            src, xf.at[rows], ssem.at[m], rsem.at[m], device_id={"space": target}, device_id_type=MESH
        )

    me_blk = idx(xh, z)
    out = {}

    def send(m, *args, **kw):
        out[m] = message(m, *args, **kw)
        out[m].start()

    def arrived(m, half):
        message(m, landing[m], half, X).wait_recv()

    landing = {
        0: idx(xo, z),
        1: idx(xh, z - 1),
        2: idx(xh, z + 1),
        3: idx(xh, z - 1),
        4: idx(xh, z + 1),
        5: idx(xo, z),
        6: idx(xo, z - 1),
        7: idx(xo, z + 1),
        8: idx(xh, z + 2),
        9: idx(xo, z - 1),
        10: idx(xo, z + 1),
        11: idx(xh, z + 2),
        12: idx(xo, z + 2),
        13: idx(xo, z + 2),
    }
    space_barrier([X, ZP, ZM])
    send(0, me_blk, 0, X, own=True)
    send(1, me_blk, 1, ZP, own=True)
    send(2, me_blk, 1, ZM, own=True)
    send(3, me_blk, 0, ZP, own=True)
    send(4, me_blk, 0, ZM, own=True)
    send(5, me_blk, 1, X, own=True)
    xf[pl.ds(me_blk * ROWS_DEV, ROWS_DEV)] = x_ref[...]
    arrived(1, 1)
    send(6, idx(xh, z - 1), 1, X)
    arrived(2, 1)
    send(7, idx(xh, z + 1), 1, X)
    send(8, idx(xh, z - way), 1, idx(xh, z + way))
    arrived(0, 0)
    send(9, idx(xo, z), 0, ZP)
    send(10, idx(xo, z), 0, ZM)
    arrived(3, 0)
    send(11, idx(xh, z - 1), 0, ZP)
    arrived(10, 0)
    send(12, idx(xo, z + 1), 0, ZM)
    arrived(8, 1)
    send(13, idx(xh, z + 2), 1, X)
    arrived(4, 0)
    arrived(9, 0)
    arrived(11, 0)
    arrived(12, 0)
    arrived(5, 1)
    arrived(6, 1)
    arrived(7, 1)
    arrived(13, 1)
    for m in range(14):
        out[m].wait_send()


def transpose_field(xf, xt):
    @pl.loop(0, ROWS // 4)
    def _(c):
        v = xf[pl.ds(c * 4, 4)].reshape(4 * COLS, CIN)
        xt[:, pl.ds(pl.multiple_of(c * (4 * COLS), 128), 4 * COLS)] = v.T


def field_mean(xf):
    def add(r, total):
        v = xf[r].astype(F32)
        return total + jnp.sum(v.reshape(COLS // 8, 8, CIN), axis=0)

    total = lax.fori_loop(0, ROWS, add, jnp.zeros((8, CIN), F32))
    return (jnp.sum(total, axis=0, keepdims=True) / FIELD).astype(BF16)


def forward(xf, w, acc, xs):
    me = lax.axis_index("space")
    base = me * ROWS_DEV
    own = xf[pl.ds(base, ROWS_DEV)].reshape(PIX, CIN)
    acc[0] = dot(own, w[0])
    for k in range(1, 4):
        acc[k] = jnp.zeros((PIX, COUT), F32)
        reach = 12 * k

        @pl.loop(0, 3)
        def _(a, k=k, reach=reach):
            start = base + (a - 1) * reach
            valid = jnp.logical_and(start + ROWS_DEV > 0, start < ROWS)

            @pl.when(valid)
            def _():
                for j in range(ROWS_DEV):
                    r = start + j
                    inside = jnp.logical_and(r >= 0, r < ROWS)
                    rc = jnp.clip(r, 0, ROWS - 1)
                    row = xf[rc]
                    xs[j * COLS : (j + 1) * COLS, :] = jnp.where(inside, row, jnp.zeros_like(row))
                for b in range(3):
                    p = dot(xs[...], w[1 + 9 * (k - 1) + 3 * a + b])
                    for j in range(ROWS_DEV):
                        lo, hi = j * COLS, (j + 1) * COLS
                        if b == 1:
                            acc[k, lo:hi, :] += p[lo:hi]
                        elif b == 0:
                            acc[k, lo + reach : hi, :] += p[lo : hi - reach]
                        else:
                            acc[k, lo : hi - reach, :] += p[lo + reach : hi]


def head(acc, mean, w_pool, lab_ref, wp, wc, cw, d_out, gp_out, gc_out, sp_out):
    pool_pre = dot(jnp.broadcast_to(mean, (16, CIN)), w_pool)[0:1]
    pool_act = jnp.broadcast_to(jax.nn.relu(pool_pre).astype(BF16), (PIX, COUT))
    acts = [jax.nn.relu(acc[k]).astype(BF16) for k in range(4)] + [pool_act]
    y_pre = dot(acts[0], wp[0:COUT])
    for k in range(1, 5):
        y_pre = y_pre + dot(acts[k], wp[k * COUT : (k + 1) * COUT])
    y_act = jax.nn.relu(y_pre).astype(BF16)
    logits = dot(y_act, wc[...])
    lane = lax.broadcasted_iota(jnp.int32, (PIX, 128), 1)
    exp_logits = jnp.where(lane < 3, jnp.exp(logits), 0.0)
    prob = exp_logits / jnp.sum(exp_logits, axis=1, keepdims=True)
    onehot = jnp.where(lane == lab_ref[...], 1.0, 0.0)
    weight = jnp.sum(onehot * cw[...], axis=1, keepdims=True)
    d_logits = ((prob - onehot) * weight * (loss_scale / FIELD)).astype(BF16)
    gc_out[...] = dot(y_act, d_logits, ((0,), (0,))).astype(BF16)
    d_y = jnp.where(y_pre > 0, dot(d_logits, wc[...], ((1,), (1,))), 0.0).astype(BF16)
    for k in range(5):
        gp_out[k * COUT : (k + 1) * COUT, :] = dot(acts[k], d_y, ((0,), (0,))).astype(BF16)
    for k in range(4):
        d_cat = dot(d_y, wp[k * COUT : (k + 1) * COUT], ((1,), (1,)))
        d_out[k] = jnp.where(acc[k] > 0, d_cat, 0.0).astype(BF16)
    d_cat = dot(d_y, wp[4 * COUT : 5 * COUT], ((1,), (1,)))
    s_pool = jnp.sum(jnp.where(pool_pre > 0, d_cat, 0.0), axis=0, keepdims=True)
    sp_out[...] = jnp.broadcast_to(s_pool, (8, COUT))


def kernel_a(x_ref, lab_ref, w_ref, wp, wc, cw, xt, d_out, gp_out, gc_out, sp_out, mean_out, xf, w, acc, xs, ssem, rsem, wsem):
    load = pltpu.make_async_copy(w_ref, w, wsem)
    load.start()
    gather_field(x_ref, xf, ssem, rsem)
    transpose_field(xf, xt)
    mean = field_mean(xf)
    mean_out[...] = jnp.broadcast_to(mean.astype(F32), (8, CIN))
    load.wait()
    forward(xf, w, acc, xs)
    head(acc, mean, w[TAPS], lab_ref, wp, wc, cw, d_out, gp_out, gc_out, sp_out)


def branch_of(tap):
    return jnp.where(tap == 0, 0, jnp.minimum((tap - 1) // 9 + 1, 3))


def share_branches(s):
    first, last = (29 * s) // 8, jnp.minimum((29 * s + 28) // 8, TAPS - 1)
    return branch_of(first), branch_of(last)


def exchange_d(d_ref, gp, gc, sp, dbuf, pbuf, cbuf, sbuf, ssem, rsem):
    me = lax.axis_index("space")
    others = [lax.rem(me + i, NS) for i in range(1, NS)]
    space_barrier(others)

    def copies(i, src_dev, t):
        k0, k1 = share_branches(t)
        rows = pl.ds(src_dev * ROWS_DEV, ROWS_DEV)

        def make(j, src, dst):
            return pltpu.make_async_remote_copy(
                src, dst, ssem.at[i, j], rsem.at[i, j], device_id={"space": t}, device_id_type=MESH
            )

        return (
            make(0, d_ref.at[k0], dbuf.at[0, rows]),
            make(1, d_ref.at[k1], dbuf.at[1, rows]),
            make(2, gp.at[pl.ds(t * PROJ_SHARE, PROJ_SHARE)], pbuf.at[src_dev]),
            make(3, gc.at[pl.ds(t * CLS_SHARE, CLS_SHARE)], cbuf.at[src_dev]),
            make(4, sp, sbuf.at[src_dev]),
        )

    for i in range(1, NS):
        t = others[i - 1]
        c = copies(i - 1, me, t)
        k0, k1 = share_branches(t)
        c[0].start()
        pl.when(k1 != k0)(c[1].start)
        c[2].start()
        c[3].start()
        c[4].start()
    k0, k1 = share_branches(me)
    mine = pl.ds(me * ROWS_DEV, ROWS_DEV)
    dbuf[0, mine] = d_ref[k0]
    dbuf[1, mine] = d_ref[k1]
    pbuf[me] = gp[pl.ds(pl.multiple_of(me * PROJ_SHARE, 32), PROJ_SHARE), :]
    cbuf[me] = gc[pl.ds(pl.multiple_of(me * CLS_SHARE, 32), CLS_SHARE), :]
    sbuf[me] = sp[...]
    for i in range(1, NS):
        src_dev = lax.rem(me - i + NS, NS)
        c = copies(i - 1, src_dev, me)
        c[0].wait_recv()
        pl.when(k1 != k0)(c[1].wait_recv)
        c[2].wait_recv()
        c[3].wait_recv()
        c[4].wait_recv()
    for i in range(1, NS):
        t = others[i - 1]
        c = copies(i - 1, me, t)
        kt0, kt1 = share_branches(t)
        c[0].wait_send()
        pl.when(kt1 != kt0)(c[1].wait_send)
        c[2].wait_send()
        c[3].wait_send()
        c[4].wait_send()


def weight_gradient(xt, dbuf, dsh, acc, o_ref):
    me = lax.axis_index("space")
    k0, _ = share_branches(me)
    first = (29 * me) // 8
    last = jnp.minimum((29 * me + 28) // 8, TAPS - 1)
    dsh[0:PAD] = jnp.zeros((PAD, COLS, COUT), BF16)
    dsh[PAD + ROWS :] = jnp.zeros((PAD, COLS, COUT), BF16)

    @pl.loop(0, 5)
    def _(ti):
        tap = first + ti

        @pl.when(tap <= last)
        def _():
            k = branch_of(tap)
            within = tap - 1 - 9 * (k - 1)
            a = jnp.where(k == 0, 1, within // 3)
            b = jnp.where(k == 0, 1, lax.rem(within + 9, 3))
            slot = jnp.where(k == k0, 0, 1)
            for kk in range(1, 4):
                for bb in (0, 2):
                    reach = 12 * kk

                    @pl.when(jnp.logical_and(k == kk, b == bb))
                    def _(bb=bb, reach=reach):
                        @pl.loop(0, ROWS)
                        def _(r):
                            v = dbuf[slot, r].astype(F32)
                            zero = jnp.zeros((reach, COUT), F32)
                            if bb == 0:
                                v = jnp.concatenate([v[reach:], zero], axis=0)
                            else:
                                v = jnp.concatenate([zero, v[: COLS - reach]], axis=0)
                            dsh[PAD + r] = v.astype(BF16)

            @pl.when(b == 1)
            def _():
                @pl.loop(0, ROWS)
                def _(r):
                    dsh[PAD + r] = dbuf[slot, r]

            off = (a - 1) * 12 * k
            lo, hi = jnp.maximum(off, 0), ROWS + jnp.minimum(off, 0)
            c_lo, c_hi = lo // 8, (hi + 7) // 8
            for half in range(2):
                row0 = tap * CIN + half * 512 - SHARE * me

                @pl.when(jnp.logical_and(row0 > -512, row0 < SHARE))
                def _(half=half, row0=row0):
                    acc[...] = jnp.zeros_like(acc)

                    def chunk(c, _):
                        px = pl.ds(pl.multiple_of(c * (8 * COLS), 128), 8 * COLS)
                        dd = dsh[pl.ds(PAD + c * 8 - off, 8)].reshape(8 * COLS, COUT)
                        acc[...] += dot(xt[half * 512 : half * 512 + 512, px], dd)
                        return 0

                    lax.fori_loop(c_lo, c_hi, chunk, 0)
                    for u in range(4):
                        at = row0 + 128 * u

                        @pl.when(jnp.logical_and(at >= 0, at < SHARE))
                        def _(u=u, at=at):
                            o_ref[pl.ds(pl.multiple_of(at, 128), 128), :] = acc[
                                128 * u : 128 * u + 128, :
                            ].astype(BF16)


def finish(o_ref, pbuf, cbuf, sbuf, mean_ref):
    me = lax.axis_index("space")
    total = pbuf[0].astype(F32)
    for s in range(1, NS):
        total = total + pbuf[s].astype(F32)
    o_ref[SHARE : SHARE + PROJ_SHARE, :] = total.astype(BF16)
    total = cbuf[0].astype(F32)
    for s in range(1, NS):
        total = total + cbuf[s].astype(F32)
    total = total.astype(BF16)
    o_ref[SHARE + PROJ_SHARE :, :] = jnp.concatenate([total, total], axis=1)

    @pl.when(me == NS - 1)
    def _():
        column = mean_ref[...].T[:, 0:1]
        total = jnp.zeros((CIN, COUT), F32)
        for s in range(NS):
            total = total + (column * sbuf[s, 0:1, :]).astype(BF16).astype(F32)
        o_ref[SHARE - CIN : SHARE, :] = total.astype(BF16)


def kernel_b(xt, d_ref, gp, gc, sp, mean_ref, o_ref, dbuf, pbuf, cbuf, sbuf, dsh, acc, ssem, rsem):
    exchange_d(d_ref, gp, gc, sp, dbuf, pbuf, cbuf, sbuf, ssem, rsem)
    weight_gradient(xt, dbuf, dsh, acc, o_ref)
    finish(o_ref, pbuf, cbuf, sbuf, mean_ref)


def per_device(features, labels, w_in, w_proj, w_cls, class_weight, matching):
    x = features[0]
    lab = labels.reshape(PIX, 1)
    wc = jnp.pad(w_cls, ((0, 0), (0, 125)))
    cw = jnp.pad(class_weight, (0, 125)).reshape(1, 128)
    vmem = pl.BlockSpec(memory_space=pltpu.VMEM)
    hbm = pl.BlockSpec(memory_space=pl.ANY)
    xt, d, gp, gc, sp, mean = pl.pallas_call(
        kernel_a,
        out_shape=(
            jax.ShapeDtypeStruct((CIN, FIELD), BF16),
            jax.ShapeDtypeStruct((4, PIX, COUT), BF16),
            jax.ShapeDtypeStruct((5 * COUT, COUT), BF16),
            jax.ShapeDtypeStruct((COUT, 128), BF16),
            jax.ShapeDtypeStruct((8, COUT), F32),
            jax.ShapeDtypeStruct((8, CIN), F32),
        ),
        in_specs=[vmem, vmem, hbm, vmem, vmem, vmem],
        out_specs=(vmem,) * 6,
        scratch_shapes=[
            pltpu.VMEM((ROWS, COLS, CIN), BF16),
            pltpu.VMEM((29, CIN, COUT), BF16),
            pltpu.VMEM((4, PIX, COUT), F32),
            pltpu.VMEM((PIX, CIN), BF16),
            pltpu.SemaphoreType.DMA((14,)),
            pltpu.SemaphoreType.DMA((14,)),
            pltpu.SemaphoreType.DMA,
        ],
        compiler_params=pltpu.CompilerParams(collective_id=0, has_side_effects=True, vmem_limit_bytes=VMEM_LIMIT),
        name="gather_forward",
    )(x, lab, w_in, w_proj, wc, cw)
    d = d.reshape(4, ROWS_DEV, COLS, COUT)
    own = pl.pallas_call(
        kernel_b,
        out_shape=jax.ShapeDtypeStruct((OUT_ROWS, COUT), BF16),
        in_specs=[vmem] * 6,
        out_specs=vmem,
        scratch_shapes=[
            pltpu.VMEM((2, ROWS, COLS, COUT), BF16),
            pltpu.VMEM((NS, PROJ_SHARE, COUT), BF16),
            pltpu.VMEM((NS, CLS_SHARE, 128), BF16),
            pltpu.VMEM((NS, 8, COUT), F32),
            pltpu.VMEM((ROWS + 2 * PAD, COLS, COUT), BF16),
            pltpu.VMEM((512, COUT), F32),
            pltpu.SemaphoreType.DMA((NS - 1, 5)),
            pltpu.SemaphoreType.DMA((NS - 1, 5)),
        ],
        compiler_params=pltpu.CompilerParams(collective_id=1, has_side_effects=True, vmem_limit_bytes=VMEM_LIMIT),
        name="exchange_gradient",
    )(xt, d, gp, gc, sp, mean)

    def swap(mask, value):
        pairs = [(r, r ^ mask) for r in range(lax.axis_size("rep"))]
        return lax.ppermute(value, "rep", pairs)

    partner = lax.switch(matching[0] - 1, [functools.partial(swap, m) for m in range(1, 16)], own)
    avg = (own.astype(F32) + partner.astype(F32)) * 0.5
    return (
        avg[None, :SHARE],
        avg[None, SHARE : SHARE + PROJ_SHARE],
        avg[None, SHARE + PROJ_SHARE :, :3],
    )


def solution(mesh):
    return jax.shard_map(
        per_device,
        mesh=mesh,
        in_specs=(P("rep", "space", None, None), P("rep", "space", None), P(), P(), P(), P(), P()),
        out_specs=(P("rep", "space", None), P("rep", "space", None), P("rep", "space", None)),
        check_vma=False,
    )
```

time: 641 us -> 206 us (0.32)
  waiting for transfers between devices: 446 us -> 44.2 us
  Pallas kernels: 0 us -> 149 us
  matrix products: 97.5 us -> 0 us
  local copies, waits for them, and re-layouts: 39.1 us -> 6.97 us
  blocking collectives: 22.7 us -> 0 us
  between operations: 14.5 us -> 0.71 us
  other arithmetic: 10.2 us -> 2.77 us
    reduce_scatter x3 -> x0, waiting for transfers between devices: 251 us -> none  [the longest x1 179 us: per_device(): lax.psum_scatter(g_in.astype(jnp.bfloat16), 'space', scatter_dimension=0,...]
    pallas_call x0 -> x2, Pallas kernels: none -> 149 us  [the longest x1 76.1 us: per_device(): pl.pallas_call(kernel_b, out_shape=jax.ShapeDtypeStruct((OUT_ROWS, COUT),...]
    dot_general x63 -> x0, matrix products: 97.5 us -> none  [the longest x27 48.2 us: per_device(): jnp.dot(row_block, w_in[1 + 9 * (k - 1) + 3 * i + j], preferred_element_t...]
    ppermute x4 -> x1, waiting for transfers between devices: 131 us -> 44.2 us  [swap(): return lax.ppermute(value, 'rep', pairs)]
    all_gather x1 -> x0, waiting for transfers between devices: 63.7 us -> none  [per_device(): whole_map = lax.all_gather(field_map, 'space', axis=0, tiled=True)]
    another operation x4 -> x0, local copies, waits for them, and re-layouts: 26.3 us -> none  [the longest x1 20.5 us: per_device(): g_in = jnp.stack(grad_list).reshape(-1, out_width)]
    psum x1 -> x0, blocking collectives: 22.7 us -> none  [per_device(): mean_in = (lax.psum(column_sum, 'space') / total_pix).astype(jnp.bfloat16)]
  transfers between devices with their start and end apart: 8 -> 1, of which waited for: 7 -> 1; matrix products, arithmetic and copies ran while one was open for 14% -> 0% of each run, Pallas kernels for 0% -> 0%
where the time goes in v1:
time: 206 us
  Pallas kernels  149 us (72%)
  waiting for transfers between devices  44.2 us (21%)
  local copies, waits for them, and re-layouts  6.97 us (3%)
  other arithmetic  2.77 us (1%)
  starting transfers between devices  2.41 us (1%)
    pallas_call x1, Pallas kernels, per_device(): pl.pallas_call(kernel_b, out_shape=jax.ShapeDtypeStruct((OUT_ROWS, COUT),...  76.1 us
    pallas_call x1, Pallas kernels, per_device(): pl.pallas_call(kernel_a, out_shape=(jax.ShapeDtypeStruct((CIN, FIELD), BF...  73.1 us
    ppermute x1, waiting for transfers between devices, swap(): return lax.ppermute(value, 'rep', pairs)  44.2 us
  transfers between devices with their start and end apart: 1, of which 1 were waited for; matrix products, arithmetic and copies ran while one was open for 0% of the time, Pallas kernels for 0%

profile of v1, /device:TPU:1, one launch (start us, length us, event | category | flops | bytes accessed | tf_op | source)
XLA Modules:
  0.0 206.2 jit_solution(11520763394888888003)
XLA Ops:
  0.6 0.7 reduce
  1.3 0.9 reshape.23.lab_ref
  2.2 0.8 copy.13
  3.0 0.6 pad.8.wc
  3.7 1.2 pad_bitcast_fusion.cw
  4.9 73.1 %gather_forward.1 = (bf16[1024,3840]{1,0:T(8,128)(2,1)}, bf16[4,480,256]{2,1,0:T(8,128)(2,1)}, bf16[1280,256]{1,0:T(8,128)(2,1)}, bf16[256,128]{1,0:T(8,128)(2,1)}, f32[8,256]{1,0:T(8,128)}, /*index=5*/f32[8,1024]{1,0:T(8,128)}) custom-call(bf16[5,96,1024]{2,1,0:T(8,128)(2,1)} %bitcast.12, s32[480,1]{1,0:T(8,128)} %reshape.23.lab_ref, ...), custom_call_target="tpu_custom_call" | custom-call | tf_op jit(solution)/shard_map/gather_forward/pallas_call | solution.py:382
  77.9 0.0 copy-start
  77.9 76.1 %exchange_gradient.1 = bf16[3904,256]{1,0:T(8,128)(2,1)S(1)} custom-call(bf16[1024,3840]{1,0:T(8,128)(2,1)} %get-tuple-element.46.xt, bf16[4,5,96,256]{3,2,1,0:T(8,128)(2,1)} %bitcast.13, bf16[1280,256]{1,0:T(8,128)(2,1)} %get-tuple-element.48.gp, bf16[256,128]{1,0:T(8,128)(2,1)} %get-tuple-element.49.gc, f32[8,256]{1,0:T(8,128)} %get-tuple-element.50.sp, ...), custom_call_target="tpu_custom_call" | custom-call | tf_op jit(solution)/shard_map/exchange_gradient/pallas_call | solution.py:407
  154.0 0.0 copy-done
  154.0 46.6 %conditional.4 = (bf16[3904,256]{1,0:T(8,128)(2,1)}) conditional(s32[]{:T(128)} %bitcast.3, bf16[3904,256]{1,0:T(8,128)(2,1)S(1)} %exchange_gradient.1, bf16[3904,256]{1,0:T(8,128)(2,1)S(1)} %exchange_gradient.1, bf16[3904,256]{1,0:T(8,128)(2,1)S(1)} %exchange_gradient.1, ...), branch_computations={%region_0.1_spmd, %region_1.2_spmd, %region_2.3_spmd, %region_3.4_... | conditional | bytes 7995440
  154.1 2.4 %collective-permute-start.4 = (bf16[3904,256]{1,0:T(8,128)(2,1)S(1)}, bf16[3904,256]{1,0:T(8,128)(2,1)}, u32[]{:S(2)}, u32[]{:S(2)}) collective-permute-start(bf16[3904,256]{1,0:T(8,128)(2,1)S(1)} %param.4), channel_id=1, source_target_pairs={{0,5},{1,4},{2,7},{3,6},{4,1},{5,0},{6,3},{7,2},{8,13},{9,12},{10,... | collective-permute-start | bytes 5996552 | tf_op jit(solution)/shard_map/cond/branch_4_fun/ppermute | solution.py:428
  156.5 44.2 %collective-permute-done.4 = bf16[3904,256]{1,0:T(8,128)(2,1)} collective-permute-done((bf16[3904,256]{1,0:T(8,128)(2,1)S(1)}, bf16[3904,256]{1,0:T(8,128)(2,1)}, u32[]{:S(2)}, u32[]{:S(2)}) %collective-permute-start.4) | collective-permute-done | bytes 1998880 | tf_op jit(solution)/shard_map/cond/branch_4_fun/ppermute | solution.py:428
  200.7 2.1 %add_multiply_fusion = f32[3904,256]{1,0:T(8,128)S(1)} fusion(bf16[3904,256]{1,0:T(8,128)(2,1)} %get-tuple-element.58, bf16[3904,256]{1,0:T(8,128)(2,1)S(1)} %exchange_gradient.1), kind=kLoop, calls=%fused_computation | loop fusion | flops 3997696 | bytes 7995392 | tf_op jit(solution)/shard_map/mul | solution.py:431
  202.8 2.1 %slice_bitcast_fusion = f32[1,3712,256]{2,1,0:T(8,128)} fusion(f32[3904,256]{1,0:T(8,128)S(1)} %add_multiply_fusion), kind=kLoop, calls=%fused_computation.1 | loop fusion | bytes 7602176 | tf_op jit(solution)/shard_map/broadcast_in_dim | solution.py:433
  204.9 0.7 slice_bitcast_fusion.1
  205.6 0.6 copy.16
  (1 shorter events, 0.0 us)
Async XLA Ops:
  77.9 76.1 %copy-start = (s32[16]{0:T(128)S(1)}, s32[16]{0:T(128)}, u32[]{:S(2)}) copy-start(s32[16]{0:T(128)} %param.28) | copy-start | bytes 196
  154.1 46.6 %collective-permute-start.4 = (bf16[3904,256]{1,0:T(8,128)(2,1)S(1)}, bf16[3904,256]{1,0:T(8,128)(2,1)}, u32[]{:S(2)}, u32[]{:S(2)}) collective-permute-start(bf16[3904,256]{1,0:T(8,128)(2,1)S(1)} %param.4), channel_id=1, source_target_pairs={{0,5},{1,4},{2,7},{3,6},{4,1},{5,0},{6,3},{7,2},{8,13},{9,12},{10,... | collective-permute-start | bytes 5996552 | tf_op jit(solution)/shard_map/cond/branch_4_fun/ppermute | solution.py:428

commit v2 on v0

v2 whole, which is shorter than its diff:
```python
import functools

import jax
import jax.numpy as jnp
from jax import lax
from jax.experimental import pallas as pl
from jax.experimental.pallas import tpu as pltpu
from jax.sharding import PartitionSpec as P

MESH = pl.DeviceIdType.MESH
F32 = jnp.float32
BF16 = jnp.bfloat16

NS = 8
ROWS_DEV = 5
ROWS = 40
COLS = 96
CIN = 1024
COUT = 256
PIX = ROWS_DEV * COLS
FIELD = ROWS * COLS
TAPS = 28
SHARE = 29 * CIN // NS
PROJ_SHARE = 5 * COUT // NS
CLS_SHARE = COUT // NS
OUT_ROWS = SHARE + PROJ_SHARE + CLS_SHARE
PAD = 4
VMEM_LIMIT = 62 * 2**20
loss_scale = 1024.0


def dot(a, b, dims=((1,), (0,))):
    return lax.dot_general(a, b, (dims, ((), ())), preferred_element_type=F32)


def place():
    sp, rep = lax.axis_index("space"), lax.axis_index("rep")
    core = lax.rem(rep, 2)
    return sp // 4, lax.rem(sp, 4), core, rep - core


def device(xh, z, core, rep0):
    return {"space": xh * 4 + lax.rem(z + 8, 4), "rep": rep0 + core}


def block_rows(block, first=0, count=ROWS_DEV):
    return pl.ds(block * ROWS_DEV + first, count)


ORDER = ((1, 0), (3, 0), (2, 0), (1, 1), (3, 1), (2, 1), (0, 1))


def entry_barrier():
    xh, z, core, rep0 = place()
    barrier = pltpu.get_barrier_semaphore()

    def signal(dev):
        pl.semaphore_signal(barrier, inc=1, device_id=dev, device_id_type=MESH)

    for dz, dc in ORDER:
        signal(device(xh, z + dz, jnp.bitwise_xor(core, dc), rep0))

    @pl.when(xh != core)
    def _():
        signal(device(core, z, xh, rep0))

    pl.semaphore_wait(barrier, 7 + jnp.where(xh != core, 1, 0))


def gather_field(x_hbm, lab_ref, xf, lab, ssem, rsem, lsem, while_waiting):
    xh, z, core, rep0 = place()
    way = 1 - 2 * core
    mine = 4 * core + z
    sibling = device(xh, z, 1 - core, rep0)

    def blk(zz, plane=core):
        return plane * 4 + lax.rem(zz + 8, 4)

    def message(m, block, first, count, target):
        rows = block_rows(block, first, count)
        return pltpu.make_async_remote_copy(
            xf.at[rows], xf.at[rows], ssem.at[m], rsem.at[m], device_id=target, device_id_type=MESH
        )

    partner = device(core, z, xh, rep0)
    swap = pltpu.make_async_remote_copy(
        x_hbm, xf.at[block_rows(4 * xh + z)], ssem.at[13], rsem.at[13], device_id=partner, device_id_type=MESH
    )
    swap_in = pltpu.make_async_remote_copy(
        x_hbm, xf.at[block_rows(mine)], ssem.at[13], rsem.at[13], device_id=partner, device_id_type=MESH
    )
    swap_lab = pltpu.make_async_remote_copy(
        lab_ref, lab, ssem.at[14], rsem.at[14], device_id=partner, device_id_type=MESH
    )
    local = pltpu.make_async_copy(x_hbm, xf.at[block_rows(mine)], lsem)

    @pl.when(xh != core)
    def _():
        swap.start()
        swap_lab.start()
        swap_in.wait_recv()
        swap_lab.wait_recv()

    @pl.when(xh == core)
    def _():
        local.start()
        lab[...] = lab_ref[...]
        local.wait()

    out = []

    def send(*args):
        c = message(*args)
        c.start()
        out.append(c)

    def arrived(m, block, first, count):
        message(m, block, first, count, sibling).wait_recv()

    ahead, behind = device(xh, z + way, core, rep0), device(xh, z - way, core, rep0)
    send(0, mine, 0, 3, ahead)
    send(1, mine, 3, 2, behind)
    send(2, mine, 3, 2, ahead)
    send(3, mine, 0, 3, behind)
    send(6, mine, 0, 5, sibling)
    while_waiting(xf)
    arrived(0, blk(z - way), 0, 3)
    send(4, blk(z - way), 0, 3, ahead)
    arrived(1, blk(z + way), 3, 2)
    send(5, blk(z + way), 3, 2, behind)
    send(7, blk(z - way), 0, 3, sibling)
    send(8, blk(z + way), 3, 2, sibling)
    arrived(2, blk(z - way), 3, 2)
    send(9, blk(z - way), 3, 2, sibling)
    arrived(3, blk(z + way), 0, 3)
    send(10, blk(z + way), 0, 3, sibling)
    arrived(5, blk(z + 2), 3, 2)
    send(11, blk(z + 2), 3, 2, sibling)
    arrived(4, blk(z + 2), 0, 3)
    send(12, blk(z + 2), 0, 3, sibling)
    other = 1 - core
    arrived(6, blk(z, other), 0, 5)
    arrived(7, blk(z + way, other), 0, 3)
    arrived(8, blk(z - way, other), 3, 2)
    arrived(9, blk(z + way, other), 3, 2)
    arrived(10, blk(z - way, other), 0, 3)
    arrived(11, blk(z + 2, other), 3, 2)
    arrived(12, blk(z + 2, other), 0, 3)

    def drain():
        for c in out:
            c.wait_send()

        @pl.when(xh != core)
        def _():
            swap.wait_send()
            swap_lab.wait_send()

    return drain


def transpose_field(xf, xt):
    @pl.loop(0, ROWS // 4)
    def _(c):
        v = xf[pl.ds(c * 4, 4)].reshape(4 * COLS, CIN)
        xt[:, pl.ds(pl.multiple_of(c * (4 * COLS), 128), 4 * COLS)] = v.T


def field_mean(xf):
    def add(r, total):
        v = xf[r].astype(F32)
        return total + jnp.sum(v.reshape(COLS // 8, 8, CIN), axis=0)

    total = lax.fori_loop(0, ROWS, add, jnp.zeros((8, CIN), F32))
    return (jnp.sum(total, axis=0, keepdims=True) / FIELD).astype(BF16)


def add_tap(acc, k, b, p, fresh=False):
    reach = 12 * k
    if b == 1:
        acc[k] = p if fresh else acc[k] + p
        return
    for j in range(ROWS_DEV):
        lo, hi = j * COLS, (j + 1) * COLS
        if b == 0:
            acc[k, lo + reach : hi, :] += p[lo : hi - reach]
        else:
            acc[k, lo : hi - reach, :] += p[lo + reach : hi]


def forward_own(xf, w, acc, base):
    own = xf[pl.ds(base, ROWS_DEV)].reshape(PIX, CIN)
    acc[0] = dot(own, w[0])
    for k in range(1, 4):
        for b in (1, 0, 2):
            add_tap(acc, k, b, dot(own, w[1 + 9 * (k - 1) + 3 + b]), fresh=True)


def forward_others(xf, w, acc, xs, base):
    for k in range(1, 4):
        reach = 12 * k

        @pl.loop(0, 2)
        def _(half, k=k, reach=reach):
            a = 2 * half
            start = base + (a - 1) * reach
            valid = jnp.logical_and(start + ROWS_DEV > 0, start < ROWS)

            @pl.when(valid)
            def _():
                for j in range(ROWS_DEV):
                    r = start + j
                    inside = jnp.logical_and(r >= 0, r < ROWS)
                    row = xf[jnp.clip(r, 0, ROWS - 1)]
                    xs[j * COLS : (j + 1) * COLS, :] = jnp.where(inside, row, jnp.zeros_like(row))
                for b in range(3):
                    add_tap(acc, k, b, dot(xs[...], w[1 + 9 * (k - 1) + 3 * a + b]))


def head(acc, mean, w_pool, lab, wp, wc, cw, d_out, gp_out, gc_out, sp_out):
    pool_pre = dot(jnp.broadcast_to(mean, (16, CIN)), w_pool)[0:1]
    pool_act = jnp.broadcast_to(jax.nn.relu(pool_pre).astype(BF16), (PIX, COUT))
    acts = [jax.nn.relu(acc[k]).astype(BF16) for k in range(4)] + [pool_act]
    y_pre = dot(acts[0], wp[0:COUT])
    for k in range(1, 5):
        y_pre = y_pre + dot(acts[k], wp[k * COUT : (k + 1) * COUT])
    y_act = jax.nn.relu(y_pre).astype(BF16)
    logits = dot(y_act, wc[...])
    lane = lax.broadcasted_iota(jnp.int32, (PIX, 128), 1)
    lab_t = lab[...].astype(F32).T
    label = jnp.concatenate([lab_t[:COLS, j : j + 1] for j in range(ROWS_DEV)], axis=0)
    exp_logits = jnp.where(lane < 3, jnp.exp(logits), 0.0)
    prob = exp_logits / jnp.sum(exp_logits, axis=1, keepdims=True)
    onehot = jnp.where(lane.astype(F32) == label, 1.0, 0.0)
    weight = jnp.sum(onehot * cw[...], axis=1, keepdims=True)
    d_logits = ((prob - onehot) * weight * (loss_scale / FIELD)).astype(BF16)
    d_y = jnp.where(y_pre > 0, dot(d_logits, wc[...], ((1,), (1,))), 0.0).astype(BF16)
    for k in range(4):
        d_cat = dot(d_y, wp[k * COUT : (k + 1) * COUT], ((1,), (1,)))
        d_out[k] = jnp.where(acc[k] > 0, d_cat, 0.0).astype(BF16).reshape(ROWS_DEV, COLS, COUT)
    d_cat = dot(d_y, wp[4 * COUT : 5 * COUT], ((1,), (1,)))
    s_pool = jnp.sum(jnp.where(pool_pre > 0, d_cat, 0.0), axis=0, keepdims=True)
    sp_out[...] = jnp.broadcast_to(s_pool, (8, COUT))
    gc_out[...] = dot(y_act, d_logits, ((0,), (0,))).astype(BF16)

    def rest():
        for k in range(5):
            gp_out[k * COUT : (k + 1) * COUT, :] = dot(acts[k], d_y, ((0,), (0,))).astype(BF16)

    return rest


def branch_of(tap):
    return jnp.where(tap == 0, 0, jnp.minimum((tap - 1) // 9 + 1, 3))


def pick(i, values):
    r = jnp.int32(values[-1])
    for j, v in enumerate(values[:-1]):
        r = jnp.where(i == j, v, r)
    return r


def share_taps(s):
    return (29 * s) // 8, jnp.minimum((29 * s + 28) // 8, TAPS - 1)


def row_blocks(slot, last_only=False):
    table = []
    for s in range(NS):
        lo, hi = (29 * s) // 8, min((29 * s + 28) // 8, TAPS - 1)
        bits = 0
        k0 = 0 if lo == 0 else (lo - 1) // 9 + 1
        for t in range(lo, hi + 1):
            k = 0 if t == 0 else (t - 1) // 9 + 1
            if (k != k0) != (slot == 1):
                continue
            a = 1 if k == 0 else (t - 1) % 9 // 3
            off = (a - 1) * 12 * k
            for h in range(ROWS):
                if 0 <= h + off < ROWS:
                    bits |= 1 << (h // ROWS_DEV)
        table.append(bits)
    return table


def wanted(slot, share, block):
    return lax.rem(lax.shift_right_logical(pick(share, row_blocks(slot)), block), 2) == 1


def d_copies(i, src_block, share, target, bufs, sems):
    d, gp, gc, sp, dbuf, pbuf, cbuf, sbuf = bufs
    ssem, rsem = sems
    lo, hi = share_taps(share)

    def make(j, src, dst):
        return pltpu.make_async_remote_copy(
            src, dst, ssem.at[i, j], rsem.at[i, j], device_id=target, device_id_type=MESH
        )

    return (
        make(0, d.at[branch_of(lo)], dbuf.at[0, block_rows(src_block)]),
        make(1, d.at[branch_of(hi)], dbuf.at[1, block_rows(src_block)]),
        make(2, gp.at[pl.ds(share * PROJ_SHARE, PROJ_SHARE)], pbuf.at[src_block]),
        make(3, gc.at[pl.ds(share * CLS_SHARE, CLS_SHARE)], cbuf.at[src_block]),
        make(4, sp, sbuf.at[src_block]),
    )


def shift_block(slot, block, rows_of, dsh):
    _, z, core, _ = place()
    first, last = share_taps(4 * core + z)
    k0 = branch_of(first)

    @pl.loop(0, 5)
    def _(ti):
        tap = first + ti
        k = branch_of(tap)
        b = jnp.where(k == 0, 1, lax.rem(tap + 2, 3))
        uses = jnp.logical_and(tap <= last, (k != k0) == (slot == 1))

        @pl.when(uses)
        def _():
            for kk in range(1, 4):
                reach = 12 * kk
                for bb in (0, 2):

                    @pl.when(jnp.logical_and(k == kk, b == bb))
                    def _(bb=bb, reach=reach):
                        @pl.loop(0, ROWS_DEV)
                        def _(j):
                            v = rows_of(j).astype(F32)
                            zero = jnp.zeros((reach, COUT), F32)
                            if bb == 0:
                                v = jnp.concatenate([v[reach:], zero], axis=0)
                            else:
                                v = jnp.concatenate([zero, v[: COLS - reach]], axis=0)
                            dsh[ti, PAD + block * ROWS_DEV + j] = v.astype(BF16)

            @pl.when(b == 1)
            def _():
                @pl.loop(0, ROWS_DEV)
                def _(j):
                    dsh[ti, PAD + block * ROWS_DEV + j] = rows_of(j)


def weight_gradient(xt, dsh, acc, o_ref):
    _, z, core, _ = place()
    share = 4 * core + z
    first, last = share_taps(share)

    @pl.loop(0, 10)
    def _(step):
        ti, half = step // 2, lax.rem(step, 2)
        tap = first + ti
        row0 = tap * CIN + half * 512 - SHARE * share
        touches = jnp.logical_and(row0 > -512, row0 < SHARE)

        @pl.when(jnp.logical_and(tap <= last, touches))
        def _():
            k = branch_of(tap)
            a = jnp.where(k == 0, 1, lax.rem(tap + 8, 9) // 3)
            off = (a - 1) * 12 * k
            lo, hi = jnp.maximum(off, 0), ROWS + jnp.minimum(off, 0)
            acc[...] = jnp.zeros_like(acc)
            m = pl.ds(pl.multiple_of(half * 512, 512), 512)

            def chunk(c, _):
                px = pl.ds(pl.multiple_of(c * (8 * COLS), 128), 8 * COLS)
                dd = dsh[ti, pl.ds(PAD + c * 8 - off, 8)].reshape(8 * COLS, COUT)
                acc[...] += dot(xt[m, px], dd)
                return 0

            lax.fori_loop(lo // 8, (hi + 7) // 8, chunk, 0)
            for u in range(4):
                at = row0 + 128 * u

                @pl.when(jnp.logical_and(at >= 0, at < SHARE))
                def _(u=u, at=at):
                    o_ref[pl.ds(pl.multiple_of(at, 128), 128), :] = acc[128 * u : 128 * u + 128, :].astype(BF16)


def finish(o_ref, pbuf, cbuf, sbuf, mean_ref, share):
    total = pbuf[0].astype(F32)
    for s in range(1, NS):
        total = total + pbuf[s].astype(F32)
    o_ref[SHARE : SHARE + PROJ_SHARE, :] = total.astype(BF16)
    total = cbuf[0].astype(F32)
    for s in range(1, NS):
        total = total + cbuf[s].astype(F32)
    total = total.astype(BF16)
    o_ref[SHARE + PROJ_SHARE :, :] = jnp.concatenate([total, total], axis=1)

    @pl.when(share == NS - 1)
    def _():
        column = mean_ref[...].T[:, 0:1]
        total = jnp.zeros((CIN, COUT), F32)
        for s in range(NS):
            total = total + (column * sbuf[s, 0:1, :]).astype(BF16).astype(F32)
        o_ref[SHARE - CIN : SHARE, :] = total.astype(BF16)


def kernel(
    x_hbm, lab_ref, w_ref, wp, wc, cw, o_ref,
    xf, w, acc, xs, lab, d, gp, gc, sp, mean_ref, xt, dbuf, pbuf, cbuf, sbuf, dsh, acc_w,
    gs, gr, ds_, dr, lsem, wsem,
):
    xh, z, core, rep0 = place()
    share = 4 * core + z
    base = share * ROWS_DEV
    load = pltpu.make_async_copy(w_ref, w, wsem)
    load.start()
    entry_barrier()

    def while_waiting(xf):
        load.wait()
        forward_own(xf, w, acc, base)
        dsh[:, 0:PAD] = jnp.zeros((5, PAD, COLS, COUT), BF16)
        dsh[:, PAD + ROWS :] = jnp.zeros((5, PAD, COLS, COUT), BF16)

    drain = gather_field(x_hbm, lab_ref, xf, lab, gs, gr, lsem, while_waiting)
    mean = field_mean(xf)
    mean_ref[...] = jnp.broadcast_to(mean.astype(F32), (8, CIN))
    forward_others(xf, w, acc, xs, base)
    rest = head(acc, mean, w[TAPS], lab, wp, wc, cw, d, gp, gc, sp)

    bufs, sems = (d, gp, gc, sp, dbuf, pbuf, cbuf, sbuf), (ds_, dr)
    sent = []
    for i, (dz, dc) in enumerate(ORDER):
        c2 = jnp.bitwise_xor(core, dc)
        z2 = lax.rem(z + dz, 4)
        t = 4 * c2 + z2
        c = d_copies(i, share, t, device(xh, z2, c2, rep0), bufs, sems)
        flags = (wanted(0, t, share), wanted(1, t, share))
        sent.append((c, flags, t))
        pl.when(flags[0])(c[0].start)
        pl.when(flags[1])(c[1].start)
    rest()
    transpose_field(xf, xt)
    for c, _, t in sent:
        c[2].start()
        c[3].start()
        pl.when(t == NS - 1)(c[4].start)

    lo, hi = share_taps(share)
    kb0, kb1 = branch_of(lo), branch_of(hi)
    pl.when(wanted(0, share, share))(lambda: shift_block(0, share, lambda j: d[kb0, j], dsh))
    pl.when(wanted(1, share, share))(lambda: shift_block(1, share, lambda j: d[kb1, j], dsh))

    def source(i):
        dz, dc = pick(i, [o[0] for o in ORDER]), pick(i, [o[1] for o in ORDER])
        c2 = jnp.bitwise_xor(core, dc)
        z2 = lax.rem(z - dz + 4, 4)
        return 4 * c2 + z2, device(xh, z2, c2, rep0)

    @pl.loop(0, NS - 1)
    def _(i):
        block, dev = source(i)
        c = d_copies(i, block, share, dev, bufs, sems)
        for slot in range(2):

            @pl.when(wanted(slot, share, block))
            def _(slot=slot):
                c[slot].wait_recv()
                shift_block(slot, block, lambda j: dbuf[slot, block * ROWS_DEV + j], dsh)

    weight_gradient(xt, dsh, acc_w, o_ref)
    pbuf[share] = gp[pl.ds(pl.multiple_of(share * PROJ_SHARE, 32), PROJ_SHARE), :]
    cbuf[share] = gc[pl.ds(pl.multiple_of(share * CLS_SHARE, 32), CLS_SHARE), :]
    sbuf[share] = sp[...]

    @pl.loop(0, NS - 1)
    def _(i):
        block, dev = source(i)
        c = d_copies(i, block, share, dev, bufs, sems)
        c[2].wait_recv()
        c[3].wait_recv()
        pl.when(share == NS - 1)(c[4].wait_recv)

    finish(o_ref, pbuf, cbuf, sbuf, mean_ref, share)
    drain()
    for c, flags, t in sent:
        pl.when(flags[0])(c[0].wait_send)
        pl.when(flags[1])(c[1].wait_send)
        c[2].wait_send()
        c[3].wait_send()
        pl.when(t == NS - 1)(c[4].wait_send)


def home(device_index, mask):
    sp, rep = device_index // 16, device_index % 16
    xh, z, core = sp // 4, sp % 4, rep % 2
    return (4 * core + z) * 16 + ((rep - core + xh) ^ mask)


def per_device(features, labels, w_in, w_proj, w_cls, class_weight, matching):
    x = features[0]
    lab = jnp.pad(labels[0], ((0, 8 - ROWS_DEV), (0, 128 - COLS)))
    wc = jnp.pad(w_cls, ((0, 0), (0, 125)))
    cw = jnp.pad(class_weight, (0, 125)).reshape(1, 128)
    vmem = pl.BlockSpec(memory_space=pltpu.VMEM)
    hbm = pl.BlockSpec(memory_space=pl.ANY)
    done = pl.pallas_call(
        kernel,
        out_shape=jax.ShapeDtypeStruct((OUT_ROWS, COUT), BF16),
        in_specs=[hbm, vmem, hbm, vmem, vmem, vmem],
        out_specs=vmem,
        scratch_shapes=[
            pltpu.VMEM((ROWS, COLS, CIN), BF16),
            pltpu.VMEM((29, CIN, COUT), BF16),
            pltpu.VMEM((4, PIX, COUT), F32),
            pltpu.VMEM((PIX, CIN), BF16),
            pltpu.VMEM((8, 128), jnp.int32),
            pltpu.VMEM((4, ROWS_DEV, COLS, COUT), BF16),
            pltpu.VMEM((5 * COUT, COUT), BF16),
            pltpu.VMEM((COUT, 128), BF16),
            pltpu.VMEM((8, COUT), F32),
            pltpu.VMEM((8, CIN), F32),
            pltpu.VMEM((CIN, FIELD), BF16),
            pltpu.VMEM((2, ROWS, COLS, COUT), BF16),
            pltpu.VMEM((NS, PROJ_SHARE, COUT), BF16),
            pltpu.VMEM((NS, CLS_SHARE, 128), BF16),
            pltpu.VMEM((NS, 8, COUT), F32),
            pltpu.VMEM((5, ROWS + 2 * PAD, COLS, COUT), BF16),
            pltpu.VMEM((512, COUT), F32),
            pltpu.SemaphoreType.DMA((15,)),
            pltpu.SemaphoreType.DMA((15,)),
            pltpu.SemaphoreType.DMA((NS - 1, 5)),
            pltpu.SemaphoreType.DMA((NS - 1, 5)),
            pltpu.SemaphoreType.DMA,
            pltpu.SemaphoreType.DMA,
        ],
        compiler_params=pltpu.CompilerParams(collective_id=0, has_side_effects=True, vmem_limit_bytes=VMEM_LIMIT),
        name="field_gradient",
    )(x, lab, w_in, w_proj, wc, cw)

    def deliver(mask, value):
        n = lax.axis_size("rep") * lax.axis_size("space")
        own = lax.ppermute(value, ("space", "rep"), [(i, home(i, 0)) for i in range(n)])
        partner = lax.ppermute(value, ("space", "rep"), [(i, home(i, mask)) for i in range(n)])
        return own, partner

    own, partner = lax.switch(matching[0] - 1, [functools.partial(deliver, m) for m in range(1, 16)], done)

    def average(lo, hi, width):
        mean = (own[lo:hi, :width].astype(F32) + partner[lo:hi, :width].astype(F32)) * 0.5
        return mean[None]

    return (
        average(0, SHARE, COUT),
        average(SHARE, SHARE + PROJ_SHARE, COUT),
        average(SHARE + PROJ_SHARE, OUT_ROWS, 3),
    )


def solution(mesh):
    return jax.shard_map(
        per_device,
        mesh=mesh,
        in_specs=(P("rep", "space", None, None), P("rep", "space", None), P(), P(), P(), P(), P()),
        out_specs=(P("rep", "space", None), P("rep", "space", None), P("rep", "space", None)),
        check_vma=False,
    )
```

time: 641 us -> 178 us (0.28)
  waiting for transfers between devices: 446 us -> 46.4 us
  Pallas kernels: 0 us -> 101 us
  matrix products: 97.5 us -> 0 us
  local copies, waits for them, and re-layouts: 39.1 us -> 11.3 us
  blocking collectives: 22.7 us -> 0 us
  between operations: 14.5 us -> 0.7 us
    reduce_scatter x3 -> x0, waiting for transfers between devices: 251 us -> none  [the longest x1 179 us: per_device(): lax.psum_scatter(g_in.astype(jnp.bfloat16), 'space', scatter_dimension=0,...]
    pallas_call x0 -> x1, Pallas kernels: none -> 101 us  [per_device(): pl.pallas_call(kernel, out_shape=jax.ShapeDtypeStruct((OUT_ROWS, COUT), B...]
    dot_general x63 -> x0, matrix products: 97.5 us -> none  [the longest x27 48.2 us: per_device(): jnp.dot(row_block, w_in[1 + 9 * (k - 1) + 3 * i + j], preferred_element_t...]
    ppermute x4 -> x2, waiting for transfers between devices: 131 us -> 46.4 us  [the longest x1 41.2 us: deliver(): lax.ppermute(value, ('space', 'rep'), [(i, home(i, 0)) for i in range(n)])]
    all_gather x1 -> x0, waiting for transfers between devices: 63.7 us -> none  [per_device(): whole_map = lax.all_gather(field_map, 'space', axis=0, tiled=True)]
    another operation x4 -> x0, local copies, waits for them, and re-layouts: 26.3 us -> none  [the longest x1 20.5 us: per_device(): g_in = jnp.stack(grad_list).reshape(-1, out_width)]
    psum x1 -> x0, blocking collectives: 22.7 us -> none  [per_device(): mean_in = (lax.psum(column_sum, 'space') / total_pix).astype(jnp.bfloat16)]
    broadcast_in_dim x0 -> x3, other arithmetic: none -> 6.84 us  [average(): return mean[None]]
  transfers between devices with their start and end apart: 8 -> 2, of which waited for: 7 -> 2; matrix products, arithmetic and copies ran while one was open for 14% -> 0% of each run, Pallas kernels for 0% -> 0%
where the time goes in v2:
time: 178 us
  Pallas kernels  101 us (57%)
  waiting for transfers between devices  46.4 us (26%)
  local copies, waits for them, and re-layouts  11.3 us (6%)
  starting transfers between devices  11 us (6%)
  other arithmetic  6.84 us (4%)
    pallas_call x1, Pallas kernels, per_device(): pl.pallas_call(kernel, out_shape=jax.ShapeDtypeStruct((OUT_ROWS, COUT), B...  101 us
    ppermute x1, waiting for transfers between devices, deliver(): lax.ppermute(value, ('space', 'rep'), [(i, home(i, 0)) for i in range(n)])  41.2 us
    ppermute x1, starting transfers between devices, deliver(): lax.ppermute(value, ('space', 'rep'), [(i, home(i, 0)) for i in range(n)])  10.2 us
    broadcast_in_dim x3, other arithmetic, average(): return mean[None]  6.84 us
    cond x2, local copies, waits for them, and re-layouts, per_device(): lax.switch(matching[0] - 1, [functools.partial(deliver, m) for m in range...  6.83 us
    ppermute x1, waiting for transfers between devices, deliver(): lax.ppermute(value, ('space', 'rep'), [(i, home(i, mask)) for i in range(...  5.16 us
  transfers between devices with their start and end apart: 2, of which 2 were waited for; matrix products, arithmetic and copies ran while one was open for 0% of the time, Pallas kernels for 0%

profile of v2, /device:TPU:1, one launch (start us, length us, event | category | flops | bytes accessed | tf_op | source)
XLA Modules:
  0.0 177.6 jit_solution(930571057992187351)
XLA Ops:
  0.6 0.8 copy.13
  1.5 0.6 pad.13.wc
  2.1 0.7 copy.19
  2.8 0.6 pad.12.lab_ref
  3.4 1.2 pad_bitcast_fusion.cw
  4.5 0.0 copy-start
  4.6 101.3 %field_gradient.1 = bf16[3904,256]{1,0:T(8,128)(2,1)S(1)} custom-call(bf16[5,96,1024]{2,1,0:T(8,128)(2,1)} %bitcast.14, s32[8,128]{1,0:T(8,128)} %pad.12.lab_ref, bf16[29,1024,256]{2,1,0:T(8,128)(2,1)} %w_ref.1, bf16[1280,256]{1,0:T(8,128)(2,1)} %wp.1, bf16[256,128]{1,0:T(8,128)(2,1)} %pad.13.wc, f32[1,128]{1,0:T(1,128)} %pad_bitcast_fusion.cw), custom_call_target="tpu_custom_call" | custom-call | tf_op jit(solution)/shard_map/field_gradient/pallas_call | solution.py:503
  105.9 0.0 copy-done
  105.9 57.5 %conditional.1 = (bf16[3904,256]{1,0:T(8,128)(2,1)}, bf16[3904,256]{1,0:T(8,128)(2,1)}) conditional(s32[]{:T(128)} %bitcast, bf16[3904,256]{1,0:T(8,128)(2,1)S(1)} %field_gradient.1, bf16[3904,256]{1,0:T(8,128)(2,1)S(1)} %field_gradient.1, bf16[3904,256]{1,0:T(8,128)(2,1)S(1)} %field_gradient.1, ...), branch_computations={%region_0.1_spmd, %region_1.2_spmd, %region_2.3_spmd, %region_3.4_... | conditional | bytes 15990880 | solution.py:543
  105.9 10.2 %collective-permute-start.10 = (bf16[3904,256]{1,0:T(8,128)(2,1)S(1)}, bf16[3904,256]{1,0:T(8,128)(2,1)}, u32[]{:S(2)}, u32[]{:S(2)}) collective-permute-start(bf16[3904,256]{1,0:T(8,128)(2,1)S(1)} %param.5), channel_id=1, source_target_pairs={{0,0},{1,64},{2,2},{3,66},{4,4},{5,68},{6,6},{7,70},{8,8},{9,72},{... | collective-permute-start | bytes 5996552 | tf_op jit(solution)/shard_map/cond/branch_5_fun/ppermute | solution.py:539
  116.1 0.8 collective-permute-start.11
  117.0 41.2 %collective-permute-done.10 = bf16[3904,256]{1,0:T(8,128)(2,1)} collective-permute-done((bf16[3904,256]{1,0:T(8,128)(2,1)S(1)}, bf16[3904,256]{1,0:T(8,128)(2,1)}, u32[]{:S(2)}, u32[]{:S(2)}) %collective-permute-start.10) | collective-permute-done | bytes 1998880 | tf_op jit(solution)/shard_map/cond/branch_5_fun/ppermute | solution.py:539
  158.2 5.2 %collective-permute-done.11 = bf16[3904,256]{1,0:T(8,128)(2,1)} collective-permute-done((bf16[3904,256]{1,0:T(8,128)(2,1)S(1)}, bf16[3904,256]{1,0:T(8,128)(2,1)}, u32[]{:S(2)}, u32[]{:S(2)}) %collective-permute-start.11) | collective-permute-done | bytes 1998880 | tf_op jit(solution)/shard_map/cond/branch_5_fun/ppermute | solution.py:540
  163.4 2.9 %copy.14 = bf16[3904,256]{0,1:T(8,128)(2,1)S(1)} copy(bf16[3904,256]{1,0:T(8,128)(2,1)} %get-tuple-element.20) | data formatting | bytes 3997696 | tf_op jit(solution)/shard_map/cond | solution.py:543
  166.2 3.9 %copy.15 = bf16[3904,256]{0,1:T(8,128)(2,1)} copy(bf16[3904,256]{1,0:T(8,128)(2,1)} %get-tuple-element.21) | data formatting | bytes 3997696 | tf_op jit(solution)/shard_map/cond | solution.py:543
  170.2 0.8 multiply_bitcast_fusion.2
  171.0 0.6 copy.16
  171.5 1.6 multiply_bitcast_fusion.1
  173.1 4.5 %multiply_bitcast_fusion = f32[1,3712,256]{2,1,0:T(8,128)} fusion(bf16[3904,256]{1,0:T(8,128)(2,1)} %get-tuple-element.21, bf16[3904,256]{1,0:T(8,128)(2,1)} %get-tuple-element.20), kind=kLoop, calls=%fused_computation | loop fusion | flops 3801088 | bytes 7602176 | tf_op jit(solution)/shard_map/broadcast_in_dim | solution.py:547
Async XLA Ops:
  4.5 101.3 %copy-start = (s32[16]{0:T(128)S(1)}, s32[16]{0:T(128)}, u32[]{:S(2)}) copy-start(s32[16]{0:T(128)} %param.28) | copy-start | bytes 196
  105.9 52.3 %collective-permute-start.10 = (bf16[3904,256]{1,0:T(8,128)(2,1)S(1)}, bf16[3904,256]{1,0:T(8,128)(2,1)}, u32[]{:S(2)}, u32[]{:S(2)}) collective-permute-start(bf16[3904,256]{1,0:T(8,128)(2,1)S(1)} %param.5), channel_id=1, source_target_pairs={{0,0},{1,64},{2,2},{3,66},{4,4},{5,68},{6,6},{7,70},{8,8},{9,72},{... | collective-permute-start | bytes 5996552 | tf_op jit(solution)/shard_map/cond/branch_5_fun/ppermute | solution.py:539
  116.1 47.2 %collective-permute-start.11 = (bf16[3904,256]{1,0:T(8,128)(2,1)S(1)}, bf16[3904,256]{1,0:T(8,128)(2,1)}, u32[]{:S(2)}, u32[]{:S(2)}) collective-permute-start(bf16[3904,256]{1,0:T(8,128)(2,1)S(1)} %param.5), channel_id=1, source_target_pairs={{0,6},{1,70},{2,4},{3,68},{4,2},{5,66},{6,0},{7,64},{8,14},{9,78},... | collective-permute-start | bytes 5996552 | tf_op jit(solution)/shard_map/cond/branch_5_fun/ppermute | solution.py:540

commit v3 on v2

--- a/solution.py
+++ b/solution.py
@@ -24,7 +24,7 @@
 PROJ_SHARE = 5 * COUT // NS
 CLS_SHARE = COUT // NS
 OUT_ROWS = SHARE + PROJ_SHARE + CLS_SHARE
-PAD = 4
+M_TILE = 1024
 VMEM_LIMIT = 62 * 2**20
 loss_scale = 1024.0
 
@@ -47,7 +47,15 @@
     return pl.ds(block * ROWS_DEV + first, count)
 
 
-ORDER = ((1, 0), (3, 0), (2, 0), (1, 1), (3, 1), (2, 1), (0, 1))
+ORDER = ((1, 0), (3, 0), (2, 0), (0, 1), (1, 1), (3, 1), (2, 1))
+
+
+def far_first(z):
+    return jnp.where(jnp.logical_or(z == 0, z == 3), 1, 0)
+
+
+def other_core(dz, late, z_target):
+    return jnp.where(dz == 0, 1, jnp.bitwise_xor(late, far_first(z_target)))
 
 
 def entry_barrier():
@@ -57,7 +65,7 @@
     def signal(dev):
         pl.semaphore_signal(barrier, inc=1, device_id=dev, device_id_type=MESH)
 
-    for dz, dc in ORDER:
+    for dz, dc in ((1, 0), (2, 0), (3, 0), (0, 1), (1, 1), (2, 1), (3, 1)):
         signal(device(xh, z + dz, jnp.bitwise_xor(core, dc), rep0))
 
     @pl.when(xh != core)
@@ -225,16 +233,20 @@
     for k in range(1, 5):
         y_pre = y_pre + dot(acts[k], wp[k * COUT : (k + 1) * COUT])
     y_act = jax.nn.relu(y_pre).astype(BF16)
-    logits = dot(y_act, wc[...])
     lane = lax.broadcasted_iota(jnp.int32, (PIX, 128), 1)
-    lab_t = lab[...].astype(F32).T
+    lab_t = jnp.concatenate([lab[...].astype(F32), jnp.zeros((8 - ROWS_DEV, COLS), F32)], axis=0)
+    lab_t = jnp.concatenate([lab_t, jnp.zeros((8, 128 - COLS), F32)], axis=1).T
+    w_cls = jnp.concatenate([wc[...], jnp.zeros((COUT, 125), BF16)], axis=1)
+    row = lax.broadcasted_iota(jnp.int32, (1, 128), 1)
+    cls_weight = jnp.where(row == 0, cw[0], jnp.where(row == 1, cw[1], jnp.where(row == 2, cw[2], 0.0)))
     label = jnp.concatenate([lab_t[:COLS, j : j + 1] for j in range(ROWS_DEV)], axis=0)
+    logits = dot(y_act, w_cls)
     exp_logits = jnp.where(lane < 3, jnp.exp(logits), 0.0)
     prob = exp_logits / jnp.sum(exp_logits, axis=1, keepdims=True)
     onehot = jnp.where(lane.astype(F32) == label, 1.0, 0.0)
-    weight = jnp.sum(onehot * cw[...], axis=1, keepdims=True)
+    weight = jnp.sum(onehot * cls_weight, axis=1, keepdims=True)
     d_logits = ((prob - onehot) * weight * (loss_scale / FIELD)).astype(BF16)
-    d_y = jnp.where(y_pre > 0, dot(d_logits, wc[...], ((1,), (1,))), 0.0).astype(BF16)
+    d_y = jnp.where(y_pre > 0, dot(d_logits, w_cls, ((1,), (1,))), 0.0).astype(BF16)
     for k in range(4):
         d_cat = dot(d_y, wp[k * COUT : (k + 1) * COUT], ((1,), (1,)))
         d_out[k] = jnp.where(acc[k] > 0, d_cat, 0.0).astype(BF16).reshape(ROWS_DEV, COLS, COUT)
@@ -265,7 +277,7 @@
     return (29 * s) // 8, jnp.minimum((29 * s + 28) // 8, TAPS - 1)
 
 
-def row_blocks(slot, last_only=False):
+def row_blocks(slot):
     table = []
     for s in range(NS):
         lo, hi = (29 * s) // 8, min((29 * s + 28) // 8, TAPS - 1)
@@ -335,49 +347,64 @@
                                 v = jnp.concatenate([v[reach:], zero], axis=0)
                             else:
                                 v = jnp.concatenate([zero, v[: COLS - reach]], axis=0)
-                            dsh[ti, PAD + block * ROWS_DEV + j] = v.astype(BF16)
+                            dsh[ti, block * ROWS_DEV + j] = v.astype(BF16)
 
             @pl.when(b == 1)
             def _():
                 @pl.loop(0, ROWS_DEV)
                 def _(j):
-                    dsh[ti, PAD + block * ROWS_DEV + j] = rows_of(j)
-
-
-def weight_gradient(xt, dsh, acc, o_ref):
+                    dsh[ti, block * ROWS_DEV + j] = rows_of(j)
+
+
+def weight_gradient(xt, dsh, acc, o_ref, plane, first_half):
     _, z, core, _ = place()
     share = 4 * core + z
     first, last = share_taps(share)
-
-    @pl.loop(0, 10)
+    parts = CIN // M_TILE
+
+    @pl.loop(0, 5 * parts)
     def _(step):
-        ti, half = step // 2, lax.rem(step, 2)
+        ti, part = step // parts, lax.rem(step, parts)
         tap = first + ti
-        row0 = tap * CIN + half * 512 - SHARE * share
-        touches = jnp.logical_and(row0 > -512, row0 < SHARE)
+        row0 = tap * CIN + part * M_TILE - SHARE * share
+        touches = jnp.logical_and(row0 > -M_TILE, row0 < SHARE)
 
         @pl.when(jnp.logical_and(tap <= last, touches))
         def _():
             k = branch_of(tap)
             a = jnp.where(k == 0, 1, lax.rem(tap + 8, 9) // 3)
             off = (a - 1) * 12 * k
-            lo, hi = jnp.maximum(off, 0), ROWS + jnp.minimum(off, 0)
-            acc[...] = jnp.zeros_like(acc)
-            m = pl.ds(pl.multiple_of(half * 512, 512), 512)
+            half_rows = ROWS // 2
+            lo = jnp.maximum(plane * half_rows, -off)
+            hi = jnp.minimum(plane * half_rows + half_rows, ROWS - off)
+            n = jnp.maximum(hi - lo, 0)
+            m = pl.ds(pl.multiple_of(part * M_TILE, M_TILE), M_TILE)
+            if first_half:
+                acc[ti, m] = jnp.zeros((M_TILE, COUT), F32)
+
+            def add(row, rows):
+                px = pl.ds(pl.multiple_of((row + off) * COLS, 128), rows * COLS)
+                dd = dsh[ti, pl.ds(row, rows)].reshape(rows * COLS, COUT)
+                acc[ti, m] += dot(xt[m, px], dd)
 
             def chunk(c, _):
-                px = pl.ds(pl.multiple_of(c * (8 * COLS), 128), 8 * COLS)
-                dd = dsh[ti, pl.ds(PAD + c * 8 - off, 8)].reshape(8 * COLS, COUT)
-                acc[...] += dot(xt[m, px], dd)
+                add(lo + c * 8, 8)
                 return 0
 
-            lax.fori_loop(lo // 8, (hi + 7) // 8, chunk, 0)
-            for u in range(4):
-                at = row0 + 128 * u
-
-                @pl.when(jnp.logical_and(at >= 0, at < SHARE))
-                def _(u=u, at=at):
-                    o_ref[pl.ds(pl.multiple_of(at, 128), 128), :] = acc[128 * u : 128 * u + 128, :].astype(BF16)
+            lax.fori_loop(0, n // 8, chunk, 0)
+
+            @pl.when(lax.rem(n, 8) == 4)
+            def _():
+                add(hi - 4, 4)
+
+            if not first_half:
+                for u in range(M_TILE // 128):
+                    at = row0 + 128 * u
+
+                    @pl.when(jnp.logical_and(at >= 0, at < SHARE))
+                    def _(u=u, at=at):
+                        src = pl.ds(pl.multiple_of(part * M_TILE + 128 * u, 128), 128)
+                        o_ref[pl.ds(pl.multiple_of(at, 128), 128), :] = acc[ti, src].astype(BF16)
 
 
 def finish(o_ref, pbuf, cbuf, sbuf, mean_ref, share):
@@ -415,8 +442,6 @@
     def while_waiting(xf):
         load.wait()
         forward_own(xf, w, acc, base)
-        dsh[:, 0:PAD] = jnp.zeros((5, PAD, COLS, COUT), BF16)
-        dsh[:, PAD + ROWS :] = jnp.zeros((5, PAD, COLS, COUT), BF16)
 
     drain = gather_field(x_hbm, lab_ref, xf, lab, gs, gr, lsem, while_waiting)
     mean = field_mean(xf)
@@ -426,9 +451,9 @@
 
     bufs, sems = (d, gp, gc, sp, dbuf, pbuf, cbuf, sbuf), (ds_, dr)
     sent = []
-    for i, (dz, dc) in enumerate(ORDER):
-        c2 = jnp.bitwise_xor(core, dc)
+    for i, (dz, late) in enumerate(ORDER):
         z2 = lax.rem(z + dz, 4)
+        c2 = jnp.bitwise_xor(core, other_core(dz, late, z2))
         t = 4 * c2 + z2
         c = d_copies(i, share, t, device(xh, z2, c2, rep0), bufs, sems)
         flags = (wanted(0, t, share), wanted(1, t, share))
@@ -448,13 +473,12 @@
     pl.when(wanted(1, share, share))(lambda: shift_block(1, share, lambda j: d[kb1, j], dsh))
 
     def source(i):
-        dz, dc = pick(i, [o[0] for o in ORDER]), pick(i, [o[1] for o in ORDER])
-        c2 = jnp.bitwise_xor(core, dc)
+        dz, late = pick(i, [o[0] for o in ORDER]), pick(i, [o[1] for o in ORDER])
+        c2 = jnp.bitwise_xor(core, other_core(dz, late, z))
         z2 = lax.rem(z - dz + 4, 4)
         return 4 * c2 + z2, device(xh, z2, c2, rep0)
 
-    @pl.loop(0, NS - 1)
-    def _(i):
+    def receive(i, _):
         block, dev = source(i)
         c = d_copies(i, block, share, dev, bufs, sems)
         for slot in range(2):
@@ -464,7 +488,13 @@
                 c[slot].wait_recv()
                 shift_block(slot, block, lambda j: dbuf[slot, block * ROWS_DEV + j], dsh)
 
-    weight_gradient(xt, dsh, acc_w, o_ref)
+        return 0
+
+    far = far_first(z)
+    lax.fori_loop(0, 3 + far, receive, 0)
+    weight_gradient(xt, dsh, acc_w, o_ref, jnp.bitwise_xor(core, far), True)
+    lax.fori_loop(3 + far, NS - 1, receive, 0)
+    weight_gradient(xt, dsh, acc_w, o_ref, jnp.bitwise_xor(1 - core, far), False)
     pbuf[share] = gp[pl.ds(pl.multiple_of(share * PROJ_SHARE, 32), PROJ_SHARE), :]
     cbuf[share] = gc[pl.ds(pl.multiple_of(share * CLS_SHARE, 32), CLS_SHARE), :]
     sbuf[share] = sp[...]
@@ -487,6 +517,16 @@
         pl.when(t == NS - 1)(c[4].wait_send)
 
 
+def average(own, partner, own_tail, partner_tail, avg_in, avg_proj, avg_cls):
+    avg_in[...] = (own[...].astype(F32) + partner[...].astype(F32)) * 0.5
+
+    @pl.when(pl.program_id(0) == 0)
+    def _():
+        mean = (own_tail[...].astype(F32) + partner_tail[...].astype(F32)) * 0.5
+        avg_proj[...] = mean[:PROJ_SHARE]
+        avg_cls[...] = mean[PROJ_SHARE:, :3]
+
+
 def home(device_index, mask):
     sp, rep = device_index // 16, device_index % 16
     xh, z, core = sp // 4, sp % 4, rep % 2
@@ -495,22 +535,19 @@
 
 def per_device(features, labels, w_in, w_proj, w_cls, class_weight, matching):
     x = features[0]
-    lab = jnp.pad(labels[0], ((0, 8 - ROWS_DEV), (0, 128 - COLS)))
-    wc = jnp.pad(w_cls, ((0, 0), (0, 125)))
-    cw = jnp.pad(class_weight, (0, 125)).reshape(1, 128)
     vmem = pl.BlockSpec(memory_space=pltpu.VMEM)
     hbm = pl.BlockSpec(memory_space=pl.ANY)
     done = pl.pallas_call(
         kernel,
         out_shape=jax.ShapeDtypeStruct((OUT_ROWS, COUT), BF16),
-        in_specs=[hbm, vmem, hbm, vmem, vmem, vmem],
+        in_specs=[hbm, vmem, hbm, vmem, vmem, pl.BlockSpec(memory_space=pltpu.SMEM)],
         out_specs=vmem,
         scratch_shapes=[
             pltpu.VMEM((ROWS, COLS, CIN), BF16),
             pltpu.VMEM((29, CIN, COUT), BF16),
             pltpu.VMEM((4, PIX, COUT), F32),
             pltpu.VMEM((PIX, CIN), BF16),
-            pltpu.VMEM((8, 128), jnp.int32),
+            pltpu.VMEM((ROWS_DEV, COLS), jnp.int32),
             pltpu.VMEM((4, ROWS_DEV, COLS, COUT), BF16),
             pltpu.VMEM((5 * COUT, COUT), BF16),
             pltpu.VMEM((COUT, 128), BF16),
@@ -521,8 +558,8 @@
             pltpu.VMEM((NS, PROJ_SHARE, COUT), BF16),
             pltpu.VMEM((NS, CLS_SHARE, 128), BF16),
             pltpu.VMEM((NS, 8, COUT), F32),
-            pltpu.VMEM((5, ROWS + 2 * PAD, COLS, COUT), BF16),
-            pltpu.VMEM((512, COUT), F32),
+            pltpu.VMEM((5, ROWS, COLS, COUT), BF16),
+            pltpu.VMEM((5, CIN, COUT), F32),
             pltpu.SemaphoreType.DMA((15,)),
             pltpu.SemaphoreType.DMA((15,)),
             pltpu.SemaphoreType.DMA((NS - 1, 5)),
@@ -532,7 +569,7 @@
         ],
         compiler_params=pltpu.CompilerParams(collective_id=0, has_side_effects=True, vmem_limit_bytes=VMEM_LIMIT),
         name="field_gradient",
-    )(x, lab, w_in, w_proj, wc, cw)
+    )(x, labels[0], w_in, w_proj, w_cls, class_weight)
 
     def deliver(mask, value):
         n = lax.axis_size("rep") * lax.axis_size("space")
@@ -542,15 +579,26 @@
 
     own, partner = lax.switch(matching[0] - 1, [functools.partial(deliver, m) for m in range(1, 16)], done)
 
-    def average(lo, hi, width):
-        mean = (own[lo:hi, :width].astype(F32) + partner[lo:hi, :width].astype(F32)) * 0.5
-        return mean[None]
-
-    return (
-        average(0, SHARE, COUT),
-        average(SHARE, SHARE + PROJ_SHARE, COUT),
-        average(SHARE + PROJ_SHARE, OUT_ROWS, 3),
-    )
+    steps = 2
+    main = pl.BlockSpec((SHARE // steps, COUT), lambda i: (i, 0))
+    tail = pl.BlockSpec((pl.Element(OUT_ROWS - SHARE), pl.Element(COUT)), lambda i: (SHARE, 0))
+    avg_in, avg_proj, avg_cls = pl.pallas_call(
+        average,
+        grid=(steps,),
+        out_shape=(
+            jax.ShapeDtypeStruct((SHARE, COUT), F32),
+            jax.ShapeDtypeStruct((PROJ_SHARE, COUT), F32),
+            jax.ShapeDtypeStruct((CLS_SHARE, 3), F32),
+        ),
+        in_specs=[main, main, tail, tail],
+        out_specs=(
+            main,
+            pl.BlockSpec((PROJ_SHARE, COUT), lambda i: (0, 0)),
+            pl.BlockSpec((CLS_SHARE, 3), lambda i: (0, 0)),
+        ),
+        name="average",
+    )(own, partner, own, partner)
+    return avg_in[None], avg_proj[None], avg_cls[None]
 
 
 def solution(mesh):

time: 178 us -> 162 us (0.910); the launches traced: 178 us -> 160 us
  local copies, waits for them, and re-layouts: 11.3 us -> 4.06 us
  other arithmetic: 6.84 us -> 0 us
  Pallas kernels: 101 us -> 97.3 us
    ppermute x1, waiting for transfers between devices: 41.2 us -> 4.64 us  [deliver(): lax.ppermute(value, ('space', 'rep'), [(i, home(i, 0)) for i in range(n)])]
    ppermute x1, waiting for transfers between devices: 5.16 us -> 40.9 us  [deliver(): lax.ppermute(value, ('space', 'rep'), [(i, home(i, mask)) for i in range(...]
    pallas_call x1, Pallas kernels: 101 us -> 93.6 us  [per_device(): pl.pallas_call(kernel, out_shape=jax.ShapeDtypeStruct((OUT_ROWS, COUT), B...]
    broadcast_in_dim x3 -> x0, other arithmetic: 6.84 us -> none  [average(): return mean[None]]
    cond x2 -> x0, local copies, waits for them, and re-layouts: 6.83 us -> none  [per_device(): lax.switch(matching[0] - 1, [functools.partial(deliver, m) for m in range...]
    ppermute x1, starting transfers between devices: 0.84 us -> 7.34 us  [deliver(): lax.ppermute(value, ('space', 'rep'), [(i, home(i, mask)) for i in range(...]
    ppermute x1, starting transfers between devices: 10.2 us -> 3.86 us  [deliver(): lax.ppermute(value, ('space', 'rep'), [(i, home(i, 0)) for i in range(n)])]
    pallas_call x0 -> x1, Pallas kernels: none -> 3.69 us  [per_device(): pl.pallas_call(average, grid=(steps,), out_shape=(jax.ShapeDtypeStruct((S...]
where the time goes in v3:
time: 162 us; the launch traced here: 160 us
  Pallas kernels  97.3 us (60%)
  waiting for transfers between devices  45.5 us (28%)
  starting transfers between devices  11.2 us (7%)
  local copies, waits for them, and re-layouts  4.06 us (3%)
    pallas_call x1, Pallas kernels, per_device(): pl.pallas_call(kernel, out_shape=jax.ShapeDtypeStruct((OUT_ROWS, COUT), B...  93.6 us
    ppermute x1, waiting for transfers between devices, deliver(): lax.ppermute(value, ('space', 'rep'), [(i, home(i, mask)) for i in range(...  40.9 us
    ppermute x1, starting transfers between devices, deliver(): lax.ppermute(value, ('space', 'rep'), [(i, home(i, mask)) for i in range(...  7.34 us
    ppermute x1, waiting for transfers between devices, deliver(): lax.ppermute(value, ('space', 'rep'), [(i, home(i, 0)) for i in range(n)])  4.64 us
    unnamed x3, local copies, waits for them, and re-layouts  4.06 us
    ppermute x1, starting transfers between devices, deliver(): lax.ppermute(value, ('space', 'rep'), [(i, home(i, 0)) for i in range(n)])  3.86 us
    pallas_call x1, Pallas kernels, per_device(): pl.pallas_call(average, grid=(steps,), out_shape=(jax.ShapeDtypeStruct((S...  3.69 us
  transfers between devices with their start and end apart: 2, of which 2 were waited for; matrix products, arithmetic and copies ran while one was open for 0% of the time, Pallas kernels for 0%

profile of v3, /device:TPU:1, one launch (start us, length us, event | category | flops | bytes accessed | tf_op | source)
XLA Modules:
  0.0 159.6 jit_solution(5897161216202483405)
XLA Ops:
  1.3 1.3 copy.17
  2.6 1.4 copy.10.wc
  4.0 93.6 %field_gradient.1 = bf16[3904,256]{1,0:T(8,128)(2,1)S(1)} custom-call(bf16[5,96,1024]{2,1,0:T(8,128)(2,1)} %bitcast.9, s32[5,96]{1,0:T(8,128)} %bitcast.10, bf16[29,1024,256]{2,1,0:T(8,128)(2,1)} %w_ref.1, bf16[1280,256]{1,0:T(8,128)(2,1)} %wp.1, bf16[256,3]{1,0:T(8,128)(2,1)} %copy.10.wc, f32[3]{0:T(128)} %cw.1), custom_call_target="tpu_custom_call" | custom-call | tf_op jit(solution)/shard_map/field_gradient/pallas_call | solution.py:540
  97.6 57.0 %conditional.1 = (bf16[3904,256]{1,0:T(8,128)(2,1)}, bf16[3904,256]{1,0:T(8,128)(2,1)}) conditional(s32[]{:T(128)} %bitcast, bf16[3904,256]{1,0:T(8,128)(2,1)S(1)} %field_gradient.1, bf16[3904,256]{1,0:T(8,128)(2,1)S(1)} %field_gradient.1, bf16[3904,256]{1,0:T(8,128)(2,1)S(1)} %field_gradient.1, ...), branch_computations={%region_0.0_spmd, %region_1.0_spmd, %region_2.0_spmd, %region_3.0_... | conditional | bytes 15990880 | solution.py:580
  97.9 7.3 %collective-permute-start.21 = (bf16[3904,256]{1,0:T(8,128)(2,1)S(1)}, bf16[3904,256]{1,0:T(8,128)(2,1)}, u32[]{:S(2)}, u32[]{:S(2)}) collective-permute-start(bf16[3904,256]{1,0:T(8,128)(2,1)S(1)} %param.10), channel_id=1, source_target_pairs={{0,11},{1,75},{2,9},{3,73},{4,15},{5,79},{6,13},{7,77},{8,3},{9,67... | collective-permute-start | bytes 5996552 | tf_op jit(solution)/shard_map/cond/branch_10_fun/ppermute | solution.py:577
  105.2 3.9 %collective-permute-start.20 = (bf16[3904,256]{1,0:T(8,128)(2,1)S(1)}, bf16[3904,256]{1,0:T(8,128)(2,1)}, u32[]{:S(2)}, u32[]{:S(2)}) collective-permute-start(bf16[3904,256]{1,0:T(8,128)(2,1)S(1)} %param.10), channel_id=1, source_target_pairs={{0,0},{1,64},{2,2},{3,66},{4,4},{5,68},{6,6},{7,70},{8,8},{9,72},{... | collective-permute-start | bytes 5996552 | tf_op jit(solution)/shard_map/cond/branch_10_fun/ppermute | solution.py:576
  109.1 40.9 %collective-permute-done.21 = bf16[3904,256]{1,0:T(8,128)(2,1)} collective-permute-done((bf16[3904,256]{1,0:T(8,128)(2,1)S(1)}, bf16[3904,256]{1,0:T(8,128)(2,1)}, u32[]{:S(2)}, u32[]{:S(2)}) %collective-permute-start.21) | collective-permute-done | bytes 1998880 | tf_op jit(solution)/shard_map/cond/branch_10_fun/ppermute | solution.py:577
  150.0 4.6 %collective-permute-done.20 = bf16[3904,256]{1,0:T(8,128)(2,1)} collective-permute-done((bf16[3904,256]{1,0:T(8,128)(2,1)S(1)}, bf16[3904,256]{1,0:T(8,128)(2,1)}, u32[]{:S(2)}, u32[]{:S(2)}) %collective-permute-start.20) | collective-permute-done | bytes 1998880 | tf_op jit(solution)/shard_map/cond/branch_10_fun/ppermute | solution.py:576
  154.6 3.7 %average.1 = (f32[3712,256]{1,0:T(8,128)}, f32[160,256]{1,0:T(8,128)}, f32[32,3]{1,0:T(8,128)}) custom-call(bf16[3904,256]{1,0:T(8,128)(2,1)} %get-tuple-element.23.own.own_tail, bf16[3904,256]{1,0:T(8,128)(2,1)} %get-tuple-element.24.partner.partner_tail, bf16[3904,256]{1,0:T(8,128)(2,1)} %get-tuple-element.23.own.own_tail, ...), custom_call_target="tpu_custom_call" | custom-call | tf_op jit(solution)/shard_map/average/pallas_call | solution.py:585
  158.3 1.4 copy.12
Async XLA Ops:
  97.9 52.1 %collective-permute-start.21 = (bf16[3904,256]{1,0:T(8,128)(2,1)S(1)}, bf16[3904,256]{1,0:T(8,128)(2,1)}, u32[]{:S(2)}, u32[]{:S(2)}) collective-permute-start(bf16[3904,256]{1,0:T(8,128)(2,1)S(1)} %param.10), channel_id=1, source_target_pairs={{0,11},{1,75},{2,9},{3,73},{4,15},{5,79},{6,13},{7,77},{8,3},{9,67... | collective-permute-start | bytes 5996552 | tf_op jit(solution)/shard_map/cond/branch_10_fun/ppermute | solution.py:577
  105.2 49.4 %collective-permute-start.20 = (bf16[3904,256]{1,0:T(8,128)(2,1)S(1)}, bf16[3904,256]{1,0:T(8,128)(2,1)}, u32[]{:S(2)}, u32[]{:S(2)}) collective-permute-start(bf16[3904,256]{1,0:T(8,128)(2,1)S(1)} %param.10), channel_id=1, source_target_pairs={{0,0},{1,64},{2,2},{3,66},{4,4},{5,68},{6,6},{7,70},{8,8},{9,72},{... | collective-permute-start | bytes 5996552 | tf_op jit(solution)/shard_map/cond/branch_10_fun/ppermute | solution.py:576

commit v4 on v3

--- a/solution.py
+++ b/solution.py
@@ -75,7 +75,7 @@
     pl.semaphore_wait(barrier, 7 + jnp.where(xh != core, 1, 0))
 
 
-def gather_field(x_hbm, lab_ref, xf, lab, ssem, rsem, lsem, while_waiting):
+def gather_field(x_hbm, lab_ref, xf, lab, ssem, rsem, lsem, while_waiting, before_last):
     xh, z, core, rep0 = place()
     way = 1 - 2 * core
     mine = 4 * core + z
@@ -142,18 +142,21 @@
     send(9, blk(z - way), 3, 2, sibling)
     arrived(3, blk(z + way), 0, 3)
     send(10, blk(z + way), 0, 3, sibling)
-    arrived(5, blk(z + 2), 3, 2)
-    send(11, blk(z + 2), 3, 2, sibling)
-    arrived(4, blk(z + 2), 0, 3)
-    send(12, blk(z + 2), 0, 3, sibling)
     other = 1 - core
     arrived(6, blk(z, other), 0, 5)
     arrived(7, blk(z + way, other), 0, 3)
     arrived(8, blk(z - way, other), 3, 2)
     arrived(9, blk(z + way, other), 3, 2)
     arrived(10, blk(z - way, other), 0, 3)
+    before_last([blk(z + i, plane) for i in (0, 1, 3) for plane in (core, other)])
+    arrived(5, blk(z + 2), 3, 2)
+    send(11, blk(z + 2), 3, 2, sibling)
+    arrived(4, blk(z + 2), 0, 3)
+    send(12, blk(z + 2), 0, 3, sibling)
     arrived(11, blk(z + 2, other), 3, 2)
     arrived(12, blk(z + 2, other), 0, 3)
+
+    last = [blk(z + 2, core), blk(z + 2, other)]
 
     def drain():
         for c in out:
@@ -164,7 +167,7 @@
             swap.wait_send()
             swap_lab.wait_send()
 
-    return drain
+    return last, drain
 
 
 def transpose_field(xf, xt):
@@ -174,13 +177,14 @@
         xt[:, pl.ds(pl.multiple_of(c * (4 * COLS), 128), 4 * COLS)] = v.T
 
 
-def field_mean(xf):
-    def add(r, total):
-        v = xf[r].astype(F32)
+def add_rows(xf, total, blocks):
+    def add(r, total, block):
+        v = xf[block * ROWS_DEV + r].astype(F32)
         return total + jnp.sum(v.reshape(COLS // 8, 8, CIN), axis=0)
 
-    total = lax.fori_loop(0, ROWS, add, jnp.zeros((8, CIN), F32))
-    return (jnp.sum(total, axis=0, keepdims=True) / FIELD).astype(BF16)
+    for block in blocks:
+        total = lax.fori_loop(0, ROWS_DEV, functools.partial(add, block=block), total)
+    return total
 
 
 def add_tap(acc, k, b, p, fresh=False):
@@ -204,8 +208,8 @@
             add_tap(acc, k, b, dot(own, w[1 + 9 * (k - 1) + 3 + b]), fresh=True)
 
 
-def forward_others(xf, w, acc, xs, base):
-    for k in range(1, 4):
+def forward_others(xf, w, acc, xs, base, rates):
+    for k in rates:
         reach = 12 * k
 
         @pl.loop(0, 2)
@@ -219,7 +223,7 @@
                 for j in range(ROWS_DEV):
                     r = start + j
                     inside = jnp.logical_and(r >= 0, r < ROWS)
-                    row = xf[jnp.clip(r, 0, ROWS - 1)]
+                    row = xf[jnp.where(inside, r, base)]
                     xs[j * COLS : (j + 1) * COLS, :] = jnp.where(inside, row, jnp.zeros_like(row))
                 for b in range(3):
                     add_tap(acc, k, b, dot(xs[...], w[1 + 9 * (k - 1) + 3 * a + b]))
@@ -234,19 +238,19 @@
         y_pre = y_pre + dot(acts[k], wp[k * COUT : (k + 1) * COUT])
     y_act = jax.nn.relu(y_pre).astype(BF16)
     lane = lax.broadcasted_iota(jnp.int32, (PIX, 128), 1)
-    lab_t = jnp.concatenate([lab[...].astype(F32), jnp.zeros((8 - ROWS_DEV, COLS), F32)], axis=0)
+    lab_t = jnp.concatenate([lab[j].astype(F32) for j in range(ROWS_DEV)] + [jnp.zeros((8 - ROWS_DEV, COLS), F32)], axis=0)
     lab_t = jnp.concatenate([lab_t, jnp.zeros((8, 128 - COLS), F32)], axis=1).T
-    w_cls = jnp.concatenate([wc[...], jnp.zeros((COUT, 125), BF16)], axis=1)
+    w_cls = jnp.concatenate([wc[...].astype(F32), jnp.zeros((125, COUT), F32)], axis=0).astype(BF16)
     row = lax.broadcasted_iota(jnp.int32, (1, 128), 1)
     cls_weight = jnp.where(row == 0, cw[0], jnp.where(row == 1, cw[1], jnp.where(row == 2, cw[2], 0.0)))
     label = jnp.concatenate([lab_t[:COLS, j : j + 1] for j in range(ROWS_DEV)], axis=0)
-    logits = dot(y_act, w_cls)
+    logits = dot(y_act, w_cls, ((1,), (1,)))
     exp_logits = jnp.where(lane < 3, jnp.exp(logits), 0.0)
     prob = exp_logits / jnp.sum(exp_logits, axis=1, keepdims=True)
     onehot = jnp.where(lane.astype(F32) == label, 1.0, 0.0)
     weight = jnp.sum(onehot * cls_weight, axis=1, keepdims=True)
     d_logits = ((prob - onehot) * weight * (loss_scale / FIELD)).astype(BF16)
-    d_y = jnp.where(y_pre > 0, dot(d_logits, w_cls, ((1,), (1,))), 0.0).astype(BF16)
+    d_y = jnp.where(y_pre > 0, dot(d_logits, w_cls), 0.0).astype(BF16)
     for k in range(4):
         d_cat = dot(d_y, wp[k * COUT : (k + 1) * COUT], ((1,), (1,)))
         d_out[k] = jnp.where(acc[k] > 0, d_cat, 0.0).astype(BF16).reshape(ROWS_DEV, COLS, COUT)
@@ -301,7 +305,7 @@
 
 
 def d_copies(i, src_block, share, target, bufs, sems):
-    d, gp, gc, sp, dbuf, pbuf, cbuf, sbuf = bufs
+    d, sp, dbuf, sbuf = bufs
     ssem, rsem = sems
     lo, hi = share_taps(share)
 
@@ -313,9 +317,7 @@
     return (
         make(0, d.at[branch_of(lo)], dbuf.at[0, block_rows(src_block)]),
         make(1, d.at[branch_of(hi)], dbuf.at[1, block_rows(src_block)]),
-        make(2, gp.at[pl.ds(share * PROJ_SHARE, PROJ_SHARE)], pbuf.at[src_block]),
-        make(3, gc.at[pl.ds(share * CLS_SHARE, CLS_SHARE)], cbuf.at[src_block]),
-        make(4, sp, sbuf.at[src_block]),
+        make(2, sp, sbuf.at[src_block]),
     )
 
 
@@ -409,11 +411,11 @@
 
 def finish(o_ref, pbuf, cbuf, sbuf, mean_ref, share):
     total = pbuf[0].astype(F32)
-    for s in range(1, NS):
+    for s in range(1, 4):
         total = total + pbuf[s].astype(F32)
     o_ref[SHARE : SHARE + PROJ_SHARE, :] = total.astype(BF16)
     total = cbuf[0].astype(F32)
-    for s in range(1, NS):
+    for s in range(1, 4):
         total = total + cbuf[s].astype(F32)
     total = total.astype(BF16)
     o_ref[SHARE + PROJ_SHARE :, :] = jnp.concatenate([total, total], axis=1)
@@ -429,8 +431,8 @@
 
 def kernel(
     x_hbm, lab_ref, w_ref, wp, wc, cw, o_ref,
-    xf, w, acc, xs, lab, d, gp, gc, sp, mean_ref, xt, dbuf, pbuf, cbuf, sbuf, dsh, acc_w,
-    gs, gr, ds_, dr, lsem, wsem,
+    xf, w, acc, xs, lab, d, gp, gc, sp, mean_ref, xt, dbuf, gp_in, gc_in, gp_sum, gc_sum, pbuf, cbuf, sbuf, dsh, acc_w,
+    gs, gr, ds_, dr, ps, pr, lsem, wsem,
 ):
     xh, z, core, rep0 = place()
     share = 4 * core + z
@@ -443,13 +445,18 @@
         load.wait()
         forward_own(xf, w, acc, base)
 
-    drain = gather_field(x_hbm, lab_ref, xf, lab, gs, gr, lsem, while_waiting)
-    mean = field_mean(xf)
+    def before_last(blocks):
+        mean_ref[...] = add_rows(xf, jnp.zeros((8, CIN), F32), blocks)
+        forward_others(xf, w, acc, xs, base, (2, 3))
+
+    last_blocks, drain = gather_field(x_hbm, lab_ref, xf, lab, gs, gr, lsem, while_waiting, before_last)
+    total = add_rows(xf, mean_ref[...], last_blocks)
+    mean = (jnp.sum(total, axis=0, keepdims=True) / FIELD).astype(BF16)
     mean_ref[...] = jnp.broadcast_to(mean.astype(F32), (8, CIN))
-    forward_others(xf, w, acc, xs, base)
+    forward_others(xf, w, acc, xs, base, (1,))
     rest = head(acc, mean, w[TAPS], lab, wp, wc, cw, d, gp, gc, sp)
 
-    bufs, sems = (d, gp, gc, sp, dbuf, pbuf, cbuf, sbuf), (ds_, dr)
+    bufs, sems = (d, sp, dbuf, sbuf), (ds_, dr)
     sent = []
     for i, (dz, late) in enumerate(ORDER):
         z2 = lax.rem(z + dz, 4)
@@ -463,9 +470,23 @@
     rest()
     transpose_field(xf, xt)
     for c, _, t in sent:
-        c[2].start()
-        c[3].start()
-        pl.when(t == NS - 1)(c[4].start)
+        pl.when(t == NS - 1)(c[2].start)
+    sibling = device(xh, z, 1 - core, rep0)
+
+    def half(rows, plane):
+        return pl.ds(pl.multiple_of(plane * rows, rows), rows)
+
+    def proj_copy(j, from_ref, to_ref, target):
+        return pltpu.make_async_remote_copy(
+            from_ref, to_ref, ps.at[j], pr.at[j], device_id=target, device_id_type=MESH
+        )
+
+    to_sibling = (
+        proj_copy(0, gp.at[half(4 * PROJ_SHARE, 1 - core)], gp_in, sibling),
+        proj_copy(1, gc.at[half(4 * CLS_SHARE, 1 - core)], gc_in, sibling),
+    )
+    for c in to_sibling:
+        c.start()
 
     lo, hi = share_taps(share)
     kb0, kb1 = branch_of(lo), branch_of(hi)
@@ -490,31 +511,46 @@
 
         return 0
 
+    for c in to_sibling:
+        c.wait_recv()
+    gp_sum[...] = (gp[half(4 * PROJ_SHARE, core), :].astype(F32) + gp_in[...].astype(F32)).astype(BF16)
+    gc_sum[...] = (gc[half(4 * CLS_SHARE, core), :].astype(F32) + gc_in[...].astype(F32)).astype(BF16)
     far = far_first(z)
     lax.fori_loop(0, 3 + far, receive, 0)
+    along_z = []
+    for i, dz in enumerate((1, 3, 2)):
+        z2 = lax.rem(z + dz, 4)
+        target = device(xh, z2, core, rep0)
+        along_z.append(proj_copy(2 + i, gp_sum.at[pl.ds(z2 * PROJ_SHARE, PROJ_SHARE)], pbuf.at[z], target))
+        along_z.append(proj_copy(5 + i, gc_sum.at[pl.ds(z2 * CLS_SHARE, CLS_SHARE)], cbuf.at[z], target))
+    for c in along_z:
+        c.start()
     weight_gradient(xt, dsh, acc_w, o_ref, jnp.bitwise_xor(core, far), True)
     lax.fori_loop(3 + far, NS - 1, receive, 0)
     weight_gradient(xt, dsh, acc_w, o_ref, jnp.bitwise_xor(1 - core, far), False)
-    pbuf[share] = gp[pl.ds(pl.multiple_of(share * PROJ_SHARE, 32), PROJ_SHARE), :]
-    cbuf[share] = gc[pl.ds(pl.multiple_of(share * CLS_SHARE, 32), CLS_SHARE), :]
+    pbuf[z] = gp_sum[pl.ds(pl.multiple_of(z * PROJ_SHARE, 32), PROJ_SHARE), :]
+    cbuf[z] = gc_sum[pl.ds(pl.multiple_of(z * CLS_SHARE, 32), CLS_SHARE), :]
     sbuf[share] = sp[...]
-
-    @pl.loop(0, NS - 1)
-    def _(i):
-        block, dev = source(i)
-        c = d_copies(i, block, share, dev, bufs, sems)
-        c[2].wait_recv()
-        c[3].wait_recv()
-        pl.when(share == NS - 1)(c[4].wait_recv)
+    for i, dz in enumerate((1, 3, 2)):
+        z2 = lax.rem(z - dz + 4, 4)
+        proj_copy(2 + i, gp_sum.at[pl.ds(0, PROJ_SHARE)], pbuf.at[z2], sibling).wait_recv()
+        proj_copy(5 + i, gc_sum.at[pl.ds(0, CLS_SHARE)], cbuf.at[z2], sibling).wait_recv()
+
+    @pl.when(share == NS - 1)
+    def _():
+        @pl.loop(0, NS - 1)
+        def _(i):
+            block, dev = source(i)
+            d_copies(i, block, share, dev, bufs, sems)[2].wait_recv()
 
     finish(o_ref, pbuf, cbuf, sbuf, mean_ref, share)
     drain()
     for c, flags, t in sent:
         pl.when(flags[0])(c[0].wait_send)
         pl.when(flags[1])(c[1].wait_send)
-        c[2].wait_send()
-        c[3].wait_send()
-        pl.when(t == NS - 1)(c[4].wait_send)
+        pl.when(t == NS - 1)(c[2].wait_send)
+    for c in to_sibling + tuple(along_z):
+        c.wait_send()
 
 
 def average(own, partner, own_tail, partner_tail, avg_in, avg_proj, avg_cls):
@@ -524,7 +560,9 @@
     def _():
         mean = (own_tail[...].astype(F32) + partner_tail[...].astype(F32)) * 0.5
         avg_proj[...] = mean[:PROJ_SHARE]
-        avg_cls[...] = mean[PROJ_SHARE:, :3]
+        by_class = mean[PROJ_SHARE:, :128].T
+        for c in range(3):
+            avg_cls[c] = by_class[c : c + 1, :]
 
 
 def home(device_index, mask):
@@ -547,7 +585,7 @@
             pltpu.VMEM((29, CIN, COUT), BF16),
             pltpu.VMEM((4, PIX, COUT), F32),
             pltpu.VMEM((PIX, CIN), BF16),
-            pltpu.VMEM((ROWS_DEV, COLS), jnp.int32),
+            pltpu.VMEM((ROWS_DEV, 1, COLS), jnp.int32),
             pltpu.VMEM((4, ROWS_DEV, COLS, COUT), BF16),
             pltpu.VMEM((5 * COUT, COUT), BF16),
             pltpu.VMEM((COUT, 128), BF16),
@@ -555,21 +593,27 @@
             pltpu.VMEM((8, CIN), F32),
             pltpu.VMEM((CIN, FIELD), BF16),
             pltpu.VMEM((2, ROWS, COLS, COUT), BF16),
-            pltpu.VMEM((NS, PROJ_SHARE, COUT), BF16),
-            pltpu.VMEM((NS, CLS_SHARE, 128), BF16),
+            pltpu.VMEM((4 * PROJ_SHARE, COUT), BF16),
+            pltpu.VMEM((4 * CLS_SHARE, 128), BF16),
+            pltpu.VMEM((4 * PROJ_SHARE, COUT), BF16),
+            pltpu.VMEM((4 * CLS_SHARE, 128), BF16),
+            pltpu.VMEM((4, PROJ_SHARE, COUT), BF16),
+            pltpu.VMEM((4, CLS_SHARE, 128), BF16),
             pltpu.VMEM((NS, 8, COUT), F32),
             pltpu.VMEM((5, ROWS, COLS, COUT), BF16),
             pltpu.VMEM((5, CIN, COUT), F32),
             pltpu.SemaphoreType.DMA((15,)),
             pltpu.SemaphoreType.DMA((15,)),
-            pltpu.SemaphoreType.DMA((NS - 1, 5)),
-            pltpu.SemaphoreType.DMA((NS - 1, 5)),
+            pltpu.SemaphoreType.DMA((NS - 1, 3)),
+            pltpu.SemaphoreType.DMA((NS - 1, 3)),
+            pltpu.SemaphoreType.DMA((8,)),
+            pltpu.SemaphoreType.DMA((8,)),
             pltpu.SemaphoreType.DMA,
             pltpu.SemaphoreType.DMA,
         ],
         compiler_params=pltpu.CompilerParams(collective_id=0, has_side_effects=True, vmem_limit_bytes=VMEM_LIMIT),
         name="field_gradient",
-    )(x, labels[0], w_in, w_proj, w_cls, class_weight)
+    )(x, labels.transpose(1, 0, 2), w_in, w_proj, w_cls.T, class_weight)
 
     def deliver(mask, value):
         n = lax.axis_size("rep") * lax.axis_size("space")
@@ -588,17 +632,17 @@
         out_shape=(
             jax.ShapeDtypeStruct((SHARE, COUT), F32),
             jax.ShapeDtypeStruct((PROJ_SHARE, COUT), F32),
-            jax.ShapeDtypeStruct((CLS_SHARE, 3), F32),
+            jax.ShapeDtypeStruct((3, 1, CLS_SHARE), F32),
         ),
         in_specs=[main, main, tail, tail],
         out_specs=(
             main,
             pl.BlockSpec((PROJ_SHARE, COUT), lambda i: (0, 0)),
-            pl.BlockSpec((CLS_SHARE, 3), lambda i: (0, 0)),
+            pl.BlockSpec((3, 1, CLS_SHARE), lambda i: (0, 0, 0)),
         ),
         name="average",
     )(own, partner, own, partner)
-    return avg_in[None], avg_proj[None], avg_cls[None]
+    return avg_in[None], avg_proj[None], avg_cls.transpose(1, 2, 0)
 
 
 def solution(mesh):

time: 162 us -> 147 us (0.907); the launches traced: 160 us -> 147 us
  local copies, waits for them, and re-layouts: 4.06 us -> 0 us
  starting transfers between devices: 11.2 us -> 7.21 us
  waiting for transfers between devices: 45.5 us -> 42.4 us
    ppermute x1, starting transfers between devices: 7.34 us -> 0.09 us  [deliver(): lax.ppermute(value, ('space', 'rep'), [(i, home(i, mask)) for i in range(...]
    ppermute x1, waiting for transfers between devices: 40.9 us -> 36.5 us  [deliver(): lax.ppermute(value, ('space', 'rep'), [(i, home(i, mask)) for i in range(...]
    unnamed x3 -> x0, local copies, waits for them, and re-layouts: 4.06 us -> none
    ppermute x1, starting transfers between devices: 3.86 us -> 7.13 us  [deliver(): lax.ppermute(value, ('space', 'rep'), [(i, home(i, 0)) for i in range(n)])]
    pallas_call x1, Pallas kernels: 93.6 us -> 92 us  [per_device(): pl.pallas_call(kernel, out_shape=jax.ShapeDtypeStruct((OUT_ROWS, COUT), B...]
where the time goes in v4:
time: 147 us
  Pallas kernels  95.7 us (65%)
  waiting for transfers between devices  42.4 us (29%)
  starting transfers between devices  7.21 us (5%)
    pallas_call x1, Pallas kernels, per_device(): pl.pallas_call(kernel, out_shape=jax.ShapeDtypeStruct((OUT_ROWS, COUT), B...  92 us
    ppermute x1, waiting for transfers between devices, deliver(): lax.ppermute(value, ('space', 'rep'), [(i, home(i, mask)) for i in range(...  36.5 us
    ppermute x1, starting transfers between devices, deliver(): lax.ppermute(value, ('space', 'rep'), [(i, home(i, 0)) for i in range(n)])  7.13 us
    ppermute x1, waiting for transfers between devices, deliver(): lax.ppermute(value, ('space', 'rep'), [(i, home(i, 0)) for i in range(n)])  5.82 us
    pallas_call x1, Pallas kernels, per_device(): pl.pallas_call(average, grid=(steps,), out_shape=(jax.ShapeDtypeStruct((S...  3.74 us
  transfers between devices with their start and end apart: 2, of which 2 were waited for; matrix products, arithmetic and copies ran while one was open for 0% of the time, Pallas kernels for 0%

profile of v4, /device:TPU:1, one launch (start us, length us, event | category | flops | bytes accessed | tf_op | source)
XLA Modules:
  0.0 146.7 jit_solution(16512746113688163924)
XLA Ops:
  1.3 92.0 %field_gradient.1 = bf16[3904,256]{1,0:T(8,128)(2,1)S(1)} custom-call(bf16[5,96,1024]{2,1,0:T(8,128)(2,1)} %bitcast.8, s32[5,1,96]{2,1,0:T(1,128)} %bitcast.9, bf16[29,1024,256]{2,1,0:T(8,128)(2,1)} %w_ref.1, bf16[1280,256]{1,0:T(8,128)(2,1)} %wp.1, bf16[3,256]{1,0:T(4,128)(2,1)} %bitcast.10, f32[3]{0:T(128)} %cw.1), custom_call_target="tpu_custom_call" | custom-call | tf_op jit(solution)/shard_map/field_gradient/pallas_call | solution.py:578
  93.3 49.6 %conditional.1 = (bf16[3904,256]{1,0:T(8,128)(2,1)}, bf16[3904,256]{1,0:T(8,128)(2,1)}) conditional(s32[]{:T(128)} %bitcast, bf16[3904,256]{1,0:T(8,128)(2,1)S(1)} %field_gradient.1, bf16[3904,256]{1,0:T(8,128)(2,1)S(1)} %field_gradient.1, bf16[3904,256]{1,0:T(8,128)(2,1)S(1)} %field_gradient.1, ...), branch_computations={%region_0.0_spmd, %region_1.0_spmd, %region_2.0_spmd, %region_3.0_... | conditional | bytes 15990880 | solution.py:624
  93.3 0.1 collective-permute-start.5
  93.4 7.1 %collective-permute-start.4 = (bf16[3904,256]{1,0:T(8,128)(2,1)S(1)}, bf16[3904,256]{1,0:T(8,128)(2,1)}, u32[]{:S(2)}, u32[]{:S(2)}) collective-permute-start(bf16[3904,256]{1,0:T(8,128)(2,1)S(1)} %param.2), channel_id=1, source_target_pairs={{0,0},{1,64},{2,2},{3,66},{4,4},{5,68},{6,6},{7,70},{8,8},{9,72},{... | collective-permute-start | bytes 5996552 | tf_op jit(solution)/shard_map/cond/branch_2_fun/ppermute | solution.py:620
  100.6 36.5 %collective-permute-done.5 = bf16[3904,256]{1,0:T(8,128)(2,1)} collective-permute-done((bf16[3904,256]{1,0:T(8,128)(2,1)S(1)}, bf16[3904,256]{1,0:T(8,128)(2,1)}, u32[]{:S(2)}, u32[]{:S(2)}) %collective-permute-start.5) | collective-permute-done | bytes 1998880 | tf_op jit(solution)/shard_map/cond/branch_2_fun/ppermute | solution.py:621
  137.1 5.8 %collective-permute-done.4 = bf16[3904,256]{1,0:T(8,128)(2,1)} collective-permute-done((bf16[3904,256]{1,0:T(8,128)(2,1)S(1)}, bf16[3904,256]{1,0:T(8,128)(2,1)}, u32[]{:S(2)}, u32[]{:S(2)}) %collective-permute-start.4) | collective-permute-done | bytes 1998880 | tf_op jit(solution)/shard_map/cond/branch_2_fun/ppermute | solution.py:620
  142.9 3.7 %average.1 = (f32[3712,256]{1,0:T(8,128)}, f32[160,256]{1,0:T(8,128)}, f32[3,1,32]{2,1,0:T(1,128)}) custom-call(bf16[3904,256]{1,0:T(8,128)(2,1)} %get-tuple-element.23.own.own_tail, bf16[3904,256]{1,0:T(8,128)(2,1)} %get-tuple-element.24.partner.partner_tail, bf16[3904,256]{1,0:T(8,128)(2,1)} %get-tuple-element.23.own.own_tail, ...), custom_call_target="tpu_custom_call" | custom-call | tf_op jit(solution)/shard_map/average/pallas_call | solution.py:629
Async XLA Ops:
  93.3 43.8 %collective-permute-start.5 = (bf16[3904,256]{1,0:T(8,128)(2,1)S(1)}, bf16[3904,256]{1,0:T(8,128)(2,1)}, u32[]{:S(2)}, u32[]{:S(2)}) collective-permute-start(bf16[3904,256]{1,0:T(8,128)(2,1)S(1)} %param.2), channel_id=1, source_target_pairs={{0,3},{1,67},{2,1},{3,65},{4,7},{5,71},{6,5},{7,69},{8,11},{9,75},... | collective-permute-start | bytes 5996552 | tf_op jit(solution)/shard_map/cond/branch_2_fun/ppermute | solution.py:621
  93.4 49.5 %collective-permute-start.4 = (bf16[3904,256]{1,0:T(8,128)(2,1)S(1)}, bf16[3904,256]{1,0:T(8,128)(2,1)}, u32[]{:S(2)}, u32[]{:S(2)}) collective-permute-start(bf16[3904,256]{1,0:T(8,128)(2,1)S(1)} %param.2), channel_id=1, source_target_pairs={{0,0},{1,64},{2,2},{3,66},{4,4},{5,68},{6,6},{7,70},{8,8},{9,72},{... | collective-permute-start | bytes 5996552 | tf_op jit(solution)/shard_map/cond/branch_2_fun/ppermute | solution.py:620

commit v5 on v4

--- a/solution.py
+++ b/solution.py
@@ -523,10 +523,10 @@
         target = device(xh, z2, core, rep0)
         along_z.append(proj_copy(2 + i, gp_sum.at[pl.ds(z2 * PROJ_SHARE, PROJ_SHARE)], pbuf.at[z], target))
         along_z.append(proj_copy(5 + i, gc_sum.at[pl.ds(z2 * CLS_SHARE, CLS_SHARE)], cbuf.at[z], target))
+    weight_gradient(xt, dsh, acc_w, o_ref, jnp.bitwise_xor(core, far), True)
+    lax.fori_loop(3 + far, NS - 1, receive, 0)
     for c in along_z:
         c.start()
-    weight_gradient(xt, dsh, acc_w, o_ref, jnp.bitwise_xor(core, far), True)
-    lax.fori_loop(3 + far, NS - 1, receive, 0)
     weight_gradient(xt, dsh, acc_w, o_ref, jnp.bitwise_xor(1 - core, far), False)
     pbuf[z] = gp_sum[pl.ds(pl.multiple_of(z * PROJ_SHARE, 32), PROJ_SHARE), :]
     cbuf[z] = gc_sum[pl.ds(pl.multiple_of(z * CLS_SHARE, 32), CLS_SHARE), :]

time: 147 us -> 147 us (level)
  starting transfers between devices: 7.21 us -> 10.2 us
  Pallas kernels: 95.7 us -> 93.8 us
    ppermute x1, starting transfers between devices: 0.09 us -> 3.8 us  [deliver(): lax.ppermute(value, ('space', 'rep'), [(i, home(i, mask)) for i in range(...]
    ppermute x1, waiting for transfers between devices: 5.82 us -> 3 us  [deliver(): lax.ppermute(value, ('space', 'rep'), [(i, home(i, 0)) for i in range(n)])]
    ppermute x1, waiting for transfers between devices: 36.5 us -> 39.3 us  [deliver(): lax.ppermute(value, ('space', 'rep'), [(i, home(i, mask)) for i in range(...]
    pallas_call x1, Pallas kernels: 92 us -> 90.1 us  [per_device(): pl.pallas_call(kernel, out_shape=jax.ShapeDtypeStruct((OUT_ROWS, COUT), B...]
where the time goes in v5:
time: 147 us; the launch traced here: 148 us
  Pallas kernels  93.8 us (64%)
  waiting for transfers between devices  42.3 us (29%)
  starting transfers between devices  10.2 us (7%)
    pallas_call x1, Pallas kernels, per_device(): pl.pallas_call(kernel, out_shape=jax.ShapeDtypeStruct((OUT_ROWS, COUT), B...  90.1 us
    ppermute x1, waiting for transfers between devices, deliver(): lax.ppermute(value, ('space', 'rep'), [(i, home(i, mask)) for i in range(...  39.3 us
    ppermute x1, starting transfers between devices, deliver(): lax.ppermute(value, ('space', 'rep'), [(i, home(i, 0)) for i in range(n)])  6.42 us
    ppermute x1, starting transfers between devices, deliver(): lax.ppermute(value, ('space', 'rep'), [(i, home(i, mask)) for i in range(...  3.8 us
    pallas_call x1, Pallas kernels, per_device(): pl.pallas_call(average, grid=(steps,), out_shape=(jax.ShapeDtypeStruct((S...  3.74 us
    ppermute x1, waiting for transfers between devices, deliver(): lax.ppermute(value, ('space', 'rep'), [(i, home(i, 0)) for i in range(n)])  3 us
  transfers between devices with their start and end apart: 2, of which 2 were waited for; matrix products, arithmetic and copies ran while one was open for 0% of the time, Pallas kernels for 0%

profile of v5, /device:TPU:1, one launch (start us, length us, event | category | flops | bytes accessed | tf_op | source)
XLA Modules:
  0.0 147.9 jit_solution(5075605210736067538)
XLA Ops:
  1.3 90.1 %field_gradient.1 = bf16[3904,256]{1,0:T(8,128)(2,1)S(1)} custom-call(bf16[5,96,1024]{2,1,0:T(8,128)(2,1)} %bitcast.8, s32[5,1,96]{2,1,0:T(1,128)} %bitcast.9, bf16[29,1024,256]{2,1,0:T(8,128)(2,1)} %w_ref.1, bf16[1280,256]{1,0:T(8,128)(2,1)} %wp.1, bf16[3,256]{1,0:T(4,128)(2,1)} %bitcast.10, f32[3]{0:T(128)} %cw.1), custom_call_target="tpu_custom_call" | custom-call | tf_op jit(solution)/shard_map/field_gradient/pallas_call | solution.py:578
  91.4 52.8 %conditional.1 = (bf16[3904,256]{1,0:T(8,128)(2,1)}, bf16[3904,256]{1,0:T(8,128)(2,1)}) conditional(s32[]{:T(128)} %bitcast, bf16[3904,256]{1,0:T(8,128)(2,1)S(1)} %field_gradient.1, bf16[3904,256]{1,0:T(8,128)(2,1)S(1)} %field_gradient.1, bf16[3904,256]{1,0:T(8,128)(2,1)S(1)} %field_gradient.1, ...), branch_computations={%region_0.0_spmd, %region_1.0_spmd, %region_2.0_spmd, %region_3.0_... | conditional | bytes 15990880 | solution.py:624
  91.6 3.8 %collective-permute-start.25 = (bf16[3904,256]{1,0:T(8,128)(2,1)S(1)}, bf16[3904,256]{1,0:T(8,128)(2,1)}, u32[]{:S(2)}, u32[]{:S(2)}) collective-permute-start(bf16[3904,256]{1,0:T(8,128)(2,1)S(1)} %param.12), channel_id=1, source_target_pairs={{0,13},{1,77},{2,15},{3,79},{4,9},{5,73},{6,11},{7,75},{8,5},{9,69... | collective-permute-start | bytes 5996552 | tf_op jit(solution)/shard_map/cond/branch_12_fun/ppermute | solution.py:621
  95.4 6.4 %collective-permute-start.24 = (bf16[3904,256]{1,0:T(8,128)(2,1)S(1)}, bf16[3904,256]{1,0:T(8,128)(2,1)}, u32[]{:S(2)}, u32[]{:S(2)}) collective-permute-start(bf16[3904,256]{1,0:T(8,128)(2,1)S(1)} %param.12), channel_id=1, source_target_pairs={{0,0},{1,64},{2,2},{3,66},{4,4},{5,68},{6,6},{7,70},{8,8},{9,72},{... | collective-permute-start | bytes 5996552 | tf_op jit(solution)/shard_map/cond/branch_12_fun/ppermute | solution.py:620
  101.8 39.3 %collective-permute-done.25 = bf16[3904,256]{1,0:T(8,128)(2,1)} collective-permute-done((bf16[3904,256]{1,0:T(8,128)(2,1)S(1)}, bf16[3904,256]{1,0:T(8,128)(2,1)}, u32[]{:S(2)}, u32[]{:S(2)}) %collective-permute-start.25) | collective-permute-done | bytes 1998880 | tf_op jit(solution)/shard_map/cond/branch_12_fun/ppermute | solution.py:621
  141.1 3.0 %collective-permute-done.24 = bf16[3904,256]{1,0:T(8,128)(2,1)} collective-permute-done((bf16[3904,256]{1,0:T(8,128)(2,1)S(1)}, bf16[3904,256]{1,0:T(8,128)(2,1)}, u32[]{:S(2)}, u32[]{:S(2)}) %collective-permute-start.24) | collective-permute-done | bytes 1998880 | tf_op jit(solution)/shard_map/cond/branch_12_fun/ppermute | solution.py:620
  144.1 3.7 %average.1 = (f32[3712,256]{1,0:T(8,128)}, f32[160,256]{1,0:T(8,128)}, f32[3,1,32]{2,1,0:T(1,128)}) custom-call(bf16[3904,256]{1,0:T(8,128)(2,1)} %get-tuple-element.23.own.own_tail, bf16[3904,256]{1,0:T(8,128)(2,1)} %get-tuple-element.24.partner.partner_tail, bf16[3904,256]{1,0:T(8,128)(2,1)} %get-tuple-element.23.own.own_tail, ...), custom_call_target="tpu_custom_call" | custom-call | tf_op jit(solution)/shard_map/average/pallas_call | solution.py:629
Async XLA Ops:
  91.6 49.5 %collective-permute-start.25 = (bf16[3904,256]{1,0:T(8,128)(2,1)S(1)}, bf16[3904,256]{1,0:T(8,128)(2,1)}, u32[]{:S(2)}, u32[]{:S(2)}) collective-permute-start(bf16[3904,256]{1,0:T(8,128)(2,1)S(1)} %param.12), channel_id=1, source_target_pairs={{0,13},{1,77},{2,15},{3,79},{4,9},{5,73},{6,11},{7,75},{8,5},{9,69... | collective-permute-start | bytes 5996552 | tf_op jit(solution)/shard_map/cond/branch_12_fun/ppermute | solution.py:621
  95.4 48.7 %collective-permute-start.24 = (bf16[3904,256]{1,0:T(8,128)(2,1)S(1)}, bf16[3904,256]{1,0:T(8,128)(2,1)}, u32[]{:S(2)}, u32[]{:S(2)}) collective-permute-start(bf16[3904,256]{1,0:T(8,128)(2,1)S(1)} %param.12), channel_id=1, source_target_pairs={{0,0},{1,64},{2,2},{3,66},{4,4},{5,68},{6,6},{7,70},{8,8},{9,72},{... | collective-permute-start | bytes 5996552 | tf_op jit(solution)/shard_map/cond/branch_12_fun/ppermute | solution.py:620
